TPU v7x, 128 devices: a whole 4x4x4 slice. The times are simulated.
128 devices in a mesh: chain: 8 (over y, core), col: 16 (over z, x).
Axes of the slice: x: 4, y: 4, z: 4, core: 2. Of those that a mesh axis runs over, the one named last changes fastest.
Arguments:
- sources: float32 [8, 64, 64, 128], P('chain', 'col'), may hold values from -6 to 6
- diag_inverse: float32 [8, 64, 128, 128], P('chain', 'col')
- factor_tiles: float32 [8, 1504, 128, 128], P('chain', 'col'), may hold values from -0.109375 to 0.109375
- tile_rows: int32 [8, 1504], P('chain', 'col'), may hold values from 0 to 63
- tile_cols: int32 [8, 1504], P('chain', 'col'), may hold values from 0 to 63, as said below
Outputs:
- solved: float32 [8, 64, 64, 128], P('chain', 'col')
- leaving: float32 [8, 64, 64, 128], P('chain', 'col')
Inputs may be any that keep to these rules, and one draw needn't show every extreme that they name: `tile_cols`: entries 94 * c to 94 * (c + 1) - 1 of a group name tile columns 4 * c to 4 * (c + 1) - 1.
All inputs are finite; a program needn't handle non-finite values.
Results may differ from a plain program's by a relative error of at most 0.00018.
Values sent between devices are 32-bit elements; how exact they have to be, the bound alone decides.
No kernel may reach another device: no remote copies, remote signals or barrier semaphores. Data moves between devices by JAX's collectives and lax.ppermute only.
A program may use at most 64 MiB of HBM per device.

v0:
```python
import jax
import jax.numpy as jnp
from jax import lax
from jax.sharding import PartitionSpec as P


def shifted(block, axis, distance):
    devices = range(lax.axis_size(axis))
    route = [(i - distance, i) for i in devices if i - distance in devices]
    return lax.ppermute(block, axis, route)


def local(sources, diag_inverse, factor_tiles, tile_rows, tile_cols):
    highest = lax.Precision.HIGHEST
    section_no = lax.axis_index("chain")
    groups = lax.axis_size("chain")
    per_device = sources.shape[1]
    source_count = sources.shape[2]
    tile_size = sources.shape[3]
    own_right = sources[0]
    inverse = diag_inverse[0]
    factor = factor_tiles[0]
    rows_index = tile_rows[0]
    local_cols = tile_cols[0] - lax.axis_index("col") * per_device
    panels = 1
    panel_width = source_count // panels
    tick_count = groups + panels - 1

    def advance(moment, state_now):
        solved, leaving, inbound = state_now
        panel_no = moment - section_no
        active = (panel_no >= 0) & (panel_no < panels)
        right_side = own_right - inbound
        current = jnp.einsum("trc,tsc->tsr", inverse, right_side, precision=highest)
        picked = jnp.take(current, local_cols, axis=0)
        products = jnp.einsum("krc,ksc->ksr", factor, picked, precision=highest)
        targets = jnp.arange(per_device * lax.axis_size("col"), dtype=jnp.int32)
        onehot = (rows_index[:, None] == targets[None, :]).astype(jnp.float32)
        shares = lax.psum_scatter(
            jnp.einsum("kt,ksr->tsr", onehot, products, precision=highest),
            "col",
            scatter_dimension=0,
            tiled=True,
        )
        received = shifted(shares, "chain", 1)
        solved = jnp.where(active, current, solved)
        leaving = jnp.where(active, shares, leaving)
        return (solved, leaving, received)

    blank = jnp.zeros((per_device, source_count, tile_size), jnp.float32)
    start_in = jnp.zeros((per_device, panel_width, tile_size), jnp.float32)
    solved, leaving, last_in = lax.fori_loop(0, tick_count, advance, (blank, blank, start_in))
    return (solved[None], leaving[None])


def solution(mesh):
    return jax.shard_map(
        local,
        mesh=mesh,
        in_specs=(
            P("chain", "col", None, None),
            P("chain", "col", None, None),
            P("chain", "col", None, None),
            P("chain", "col"),
            P("chain", "col"),
        ),
        out_specs=(P("chain", "col", None, None), P("chain", "col", None, None)),
        check_vma=False,
    )
```

profile of v0, /device:TPU:1, one launch (start us, length us, event | category | flops | bytes accessed | tf_op | source)
XLA Modules:
  0.0 850.4 jit_solution(17722572304397574629)
XLA Ops:
  7.8 835.0 %while.18 = (s32[]{:T(128)}, f32[4,64,128]{2,1,0:T(8,128)S(1)}, f32[4,64,128]{2,1,0:T(8,128)S(1)}, f32[4,64,128]{2,1,0:T(8,128)S(1)}, s32[]{:T(128)}, /*index=5*...) while((s32[]{:T(128)}, f32[4,64,128]{2,1,0:T(8,128)S(1)}, ...), condition=%wide.region_2.3_spmd.clone, body=%wide.region_0.2_spmd.clone.sunk | while | flops 1825464064 | bytes 37429424 | solution.py:52
  11.0 13.7 %fusion.29 = f32[94,64,128]{2,1,0:T(8,128)S(1)} fusion(f32[94,128,128]{2,1,0:T(8,128)} %get-tuple-element.327, f32[94,64,128]{2,1,0:T(8,128)S(1)} %gather_fusion, pred[94]{0:T(512)(128)(4,1)S(1)} %compare_and_fusion.2), kind=kOutput, calls=%fused_computation.3.clone.1 | convolution fusion | flops 1183563776 | bytes 12320862 | tf_op jit(solution)/shard_map/while/body/eval_jaxpr/krc,ksc->ksr/dot_general | solution.py:36
  24.7 3.3 fusion.30
  28.1 2.6 copy.14
  30.7 77.0 %reduce-scatter.2.cloned.1.call-done = f32[4,64,128]{2,1,0:T(8,128)} async-done(((f32[64,64,128]{2,1,0:T(8,128)}), f32[4,64,128]{2,1,0:T(8,128)}) %reduce-scatter.2.cloned.1.call-update) | async-done | bytes 131088 | tf_op jit(solution)/shard_map/while/body/eval_jaxpr/reduce_scatter | solution.py:39
  107.7 5.3 collective-permute-start
  113.0 2.2 collective-permute-done
  118.3 13.7 %fusion.29 = f32[94,64,128]{2,1,0:T(8,128)S(1)} fusion(f32[94,128,128]{2,1,0:T(8,128)} %get-tuple-element.327, f32[94,64,128]{2,1,0:T(8,128)S(1)} %gather_fusion, pred[94]{0:T(512)(128)(4,1)S(1)} %compare_and_fusion.2), kind=kOutput, calls=%fused_computation.3.clone.1 | convolution fusion | flops 1183563776 | bytes 12320862 | tf_op jit(solution)/shard_map/while/body/eval_jaxpr/krc,ksc->ksr/dot_general | solution.py:36
  132.0 3.3 fusion.30
  135.3 2.6 copy.14
  137.9 73.7 %reduce-scatter.2.cloned.1.call-done = f32[4,64,128]{2,1,0:T(8,128)} async-done(((f32[64,64,128]{2,1,0:T(8,128)}), f32[4,64,128]{2,1,0:T(8,128)}) %reduce-scatter.2.cloned.1.call-update) | async-done | bytes 131088 | tf_op jit(solution)/shard_map/while/body/eval_jaxpr/reduce_scatter | solution.py:39
  211.6 5.3 collective-permute-start
  222.3 13.7 %fusion.29 = f32[94,64,128]{2,1,0:T(8,128)S(1)} fusion(f32[94,128,128]{2,1,0:T(8,128)} %get-tuple-element.327, f32[94,64,128]{2,1,0:T(8,128)S(1)} %gather_fusion, pred[94]{0:T(512)(128)(4,1)S(1)} %compare_and_fusion.2), kind=kOutput, calls=%fused_computation.3.clone.1 | convolution fusion | flops 1183563776 | bytes 12320862 | tf_op jit(solution)/shard_map/while/body/eval_jaxpr/krc,ksc->ksr/dot_general | solution.py:36
  236.0 3.3 fusion.30
  239.3 2.6 copy.14
  241.9 73.6 %reduce-scatter.2.cloned.1.call-done = f32[4,64,128]{2,1,0:T(8,128)} async-done(((f32[64,64,128]{2,1,0:T(8,128)}), f32[4,64,128]{2,1,0:T(8,128)}) %reduce-scatter.2.cloned.1.call-update) | async-done | bytes 131088 | tf_op jit(solution)/shard_map/while/body/eval_jaxpr/reduce_scatter | solution.py:39
  315.6 5.3 collective-permute-start
  320.9 2.2 collective-permute-done
  326.2 13.7 %fusion.29 = f32[94,64,128]{2,1,0:T(8,128)S(1)} fusion(f32[94,128,128]{2,1,0:T(8,128)} %get-tuple-element.327, f32[94,64,128]{2,1,0:T(8,128)S(1)} %gather_fusion, pred[94]{0:T(512)(128)(4,1)S(1)} %compare_and_fusion.2), kind=kOutput, calls=%fused_computation.3.clone.1 | convolution fusion | flops 1183563776 | bytes 12320862 | tf_op jit(solution)/shard_map/while/body/eval_jaxpr/krc,ksc->ksr/dot_general | solution.py:36
  339.9 3.3 fusion.30
  343.2 2.6 copy.14
  345.8 73.6 %reduce-scatter.2.cloned.1.call-done = f32[4,64,128]{2,1,0:T(8,128)} async-done(((f32[64,64,128]{2,1,0:T(8,128)}), f32[4,64,128]{2,1,0:T(8,128)}) %reduce-scatter.2.cloned.1.call-update) | async-done | bytes 131088 | tf_op jit(solution)/shard_map/while/body/eval_jaxpr/reduce_scatter | solution.py:39
  419.4 5.3 collective-permute-start
  424.8 2.2 collective-permute-done
  430.1 13.7 %fusion.29 = f32[94,64,128]{2,1,0:T(8,128)S(1)} fusion(f32[94,128,128]{2,1,0:T(8,128)} %get-tuple-element.327, f32[94,64,128]{2,1,0:T(8,128)S(1)} %gather_fusion, pred[94]{0:T(512)(128)(4,1)S(1)} %compare_and_fusion.2), kind=kOutput, calls=%fused_computation.3.clone.1 | convolution fusion | flops 1183563776 | bytes 12320862 | tf_op jit(solution)/shard_map/while/body/eval_jaxpr/krc,ksc->ksr/dot_general | solution.py:36
  443.8 3.3 fusion.30
  447.1 2.6 copy.14
  449.7 73.6 %reduce-scatter.2.cloned.1.call-done = f32[4,64,128]{2,1,0:T(8,128)} async-done(((f32[64,64,128]{2,1,0:T(8,128)}), f32[4,64,128]{2,1,0:T(8,128)}) %reduce-scatter.2.cloned.1.call-update) | async-done | bytes 131088 | tf_op jit(solution)/shard_map/while/body/eval_jaxpr/reduce_scatter | solution.py:39
  523.4 5.3 collective-permute-start
  528.7 2.2 collective-permute-done
  534.0 13.7 %fusion.29 = f32[94,64,128]{2,1,0:T(8,128)S(1)} fusion(f32[94,128,128]{2,1,0:T(8,128)} %get-tuple-element.327, f32[94,64,128]{2,1,0:T(8,128)S(1)} %gather_fusion, pred[94]{0:T(512)(128)(4,1)S(1)} %compare_and_fusion.2), kind=kOutput, calls=%fused_computation.3.clone.1 | convolution fusion | flops 1183563776 | bytes 12320862 | tf_op jit(solution)/shard_map/while/body/eval_jaxpr/krc,ksc->ksr/dot_general | solution.py:36
  547.7 3.3 fusion.30
  551.0 2.6 copy.14
  553.6 73.7 %reduce-scatter.2.cloned.1.call-done = f32[4,64,128]{2,1,0:T(8,128)} async-done(((f32[64,64,128]{2,1,0:T(8,128)}), f32[4,64,128]{2,1,0:T(8,128)}) %reduce-scatter.2.cloned.1.call-update) | async-done | bytes 131088 | tf_op jit(solution)/shard_map/while/body/eval_jaxpr/reduce_scatter | solution.py:39
  627.3 5.3 collective-permute-start
  632.6 2.2 collective-permute-done
  638.0 13.7 %fusion.29 = f32[94,64,128]{2,1,0:T(8,128)S(1)} fusion(f32[94,128,128]{2,1,0:T(8,128)} %get-tuple-element.327, f32[94,64,128]{2,1,0:T(8,128)S(1)} %gather_fusion, pred[94]{0:T(512)(128)(4,1)S(1)} %compare_and_fusion.2), kind=kOutput, calls=%fused_computation.3.clone.1 | convolution fusion | flops 1183563776 | bytes 12320862 | tf_op jit(solution)/shard_map/while/body/eval_jaxpr/krc,ksc->ksr/dot_general | solution.py:36
  651.7 3.3 fusion.30
  655.0 2.6 copy.14
  657.6 73.7 %reduce-scatter.2.cloned.1.call-done = f32[4,64,128]{2,1,0:T(8,128)} async-done(((f32[64,64,128]{2,1,0:T(8,128)}), f32[4,64,128]{2,1,0:T(8,128)}) %reduce-scatter.2.cloned.1.call-update) | async-done | bytes 131088 | tf_op jit(solution)/shard_map/while/body/eval_jaxpr/reduce_scatter | solution.py:39
  731.2 5.3 collective-permute-start
  736.6 2.2 collective-permute-done
  741.9 13.7 %fusion.29 = f32[94,64,128]{2,1,0:T(8,128)S(1)} fusion(f32[94,128,128]{2,1,0:T(8,128)} %get-tuple-element.327, f32[94,64,128]{2,1,0:T(8,128)S(1)} %gather_fusion, pred[94]{0:T(512)(128)(4,1)S(1)} %compare_and_fusion.2), kind=kOutput, calls=%fused_computation.3.clone.1 | convolution fusion | flops 1183563776 | bytes 12320862 | tf_op jit(solution)/shard_map/while/body/eval_jaxpr/krc,ksc->ksr/dot_general | solution.py:36
  755.6 3.3 fusion.30
  758.9 2.6 copy.14
  761.5 73.8 %reduce-scatter.2.cloned.1.call-done = f32[4,64,128]{2,1,0:T(8,128)} async-done(((f32[64,64,128]{2,1,0:T(8,128)}), f32[4,64,128]{2,1,0:T(8,128)}) %reduce-scatter.2.cloned.1.call-update) | async-done | bytes 131088 | tf_op jit(solution)/shard_map/while/body/eval_jaxpr/reduce_scatter | solution.py:39
  835.3 5.3 collective-permute-start
  840.6 2.2 collective-permute-done
  (121 shorter events, 28.7 us)
Async XLA Ops:
  7.9 99.8 %reduce-scatter.2.cloned.1.call-start = ((), (), s32[]{:S(2)}) async-start(), calls=%async_computation.1 | async-start | bytes 2228224 | tf_op jit(solution)/shard_map/while/body/eval_jaxpr/reduce_scatter | solution.py:39
  9.6 0.7 copy-start.1
  11.0 13.7 %copy-start.4 = (s32[1,94]{1,0:T(1,128)S(1)}, s32[1,94]{1,0:T(1,128)}, u32[]{:S(2)}) copy-start(s32[1,94]{1,0:T(1,128)} %get-tuple-element.325) | copy-start | bytes 1132 | tf_op jit(solution)/shard_map/while
  28.1 87.1 %copy-start.2 = (f32[4,64,128]{2,1,0:T(8,128)S(1)}, f32[4,64,128]{2,1,0:T(8,128)}, u32[]{:S(2)}) copy-start(f32[4,64,128]{2,1,0:T(8,128)} %copy-done.1) | copy-start | bytes 393220 | tf_op jit(solution)/shard_map/while
  107.7 7.5 collective-permute-start
  115.2 96.4 %reduce-scatter.2.cloned.1.call-start = ((), (), s32[]{:S(2)}) async-start(), calls=%async_computation.1 | async-start | bytes 2228224 | tf_op jit(solution)/shard_map/while/body/eval_jaxpr/reduce_scatter | solution.py:39
  116.9 0.7 copy-start.1
  118.3 13.7 %copy-start.4 = (s32[1,94]{1,0:T(1,128)S(1)}, s32[1,94]{1,0:T(1,128)}, u32[]{:S(2)}) copy-start(s32[1,94]{1,0:T(1,128)} %get-tuple-element.325) | copy-start | bytes 1132 | tf_op jit(solution)/shard_map/while
  135.3 83.9 %copy-start.2 = (f32[4,64,128]{2,1,0:T(8,128)S(1)}, f32[4,64,128]{2,1,0:T(8,128)}, u32[]{:S(2)}) copy-start(f32[4,64,128]{2,1,0:T(8,128)} %copy-done.1) | copy-start | bytes 393220 | tf_op jit(solution)/shard_map/while
  211.6 7.6 collective-permute-start
  219.2 96.4 %reduce-scatter.2.cloned.1.call-start = ((), (), s32[]{:S(2)}) async-start(), calls=%async_computation.1 | async-start | bytes 2228224 | tf_op jit(solution)/shard_map/while/body/eval_jaxpr/reduce_scatter | solution.py:39
  220.9 0.7 copy-start.1
  222.3 13.7 %copy-start.4 = (s32[1,94]{1,0:T(1,128)S(1)}, s32[1,94]{1,0:T(1,128)}, u32[]{:S(2)}) copy-start(s32[1,94]{1,0:T(1,128)} %get-tuple-element.325) | copy-start | bytes 1132 | tf_op jit(solution)/shard_map/while
  239.3 83.8 %copy-start.2 = (f32[4,64,128]{2,1,0:T(8,128)S(1)}, f32[4,64,128]{2,1,0:T(8,128)}, u32[]{:S(2)}) copy-start(f32[4,64,128]{2,1,0:T(8,128)} %copy-done.1) | copy-start | bytes 393220 | tf_op jit(solution)/shard_map/while
  315.6 7.5 collective-permute-start
  323.1 96.4 %reduce-scatter.2.cloned.1.call-start = ((), (), s32[]{:S(2)}) async-start(), calls=%async_computation.1 | async-start | bytes 2228224 | tf_op jit(solution)/shard_map/while/body/eval_jaxpr/reduce_scatter | solution.py:39
  324.8 0.7 copy-start.1
  326.2 13.7 %copy-start.4 = (s32[1,94]{1,0:T(1,128)S(1)}, s32[1,94]{1,0:T(1,128)}, u32[]{:S(2)}) copy-start(s32[1,94]{1,0:T(1,128)} %get-tuple-element.325) | copy-start | bytes 1132 | tf_op jit(solution)/shard_map/while
  343.2 83.8 %copy-start.2 = (f32[4,64,128]{2,1,0:T(8,128)S(1)}, f32[4,64,128]{2,1,0:T(8,128)}, u32[]{:S(2)}) copy-start(f32[4,64,128]{2,1,0:T(8,128)} %copy-done.1) | copy-start | bytes 393220 | tf_op jit(solution)/shard_map/while
  419.4 7.6 collective-permute-start
  427.0 96.4 %reduce-scatter.2.cloned.1.call-start = ((), (), s32[]{:S(2)}) async-start(), calls=%async_computation.1 | async-start | bytes 2228224 | tf_op jit(solution)/shard_map/while/body/eval_jaxpr/reduce_scatter | solution.py:39
  428.7 0.7 copy-start.1
  430.1 13.7 %copy-start.4 = (s32[1,94]{1,0:T(1,128)S(1)}, s32[1,94]{1,0:T(1,128)}, u32[]{:S(2)}) copy-start(s32[1,94]{1,0:T(1,128)} %get-tuple-element.325) | copy-start | bytes 1132 | tf_op jit(solution)/shard_map/while
  447.1 83.8 %copy-start.2 = (f32[4,64,128]{2,1,0:T(8,128)S(1)}, f32[4,64,128]{2,1,0:T(8,128)}, u32[]{:S(2)}) copy-start(f32[4,64,128]{2,1,0:T(8,128)} %copy-done.1) | copy-start | bytes 393220 | tf_op jit(solution)/shard_map/while
  523.4 7.5 collective-permute-start
  530.9 96.4 %reduce-scatter.2.cloned.1.call-start = ((), (), s32[]{:S(2)}) async-start(), calls=%async_computation.1 | async-start | bytes 2228224 | tf_op jit(solution)/shard_map/while/body/eval_jaxpr/reduce_scatter | solution.py:39
  532.6 0.7 copy-start.1
  534.0 13.7 %copy-start.4 = (s32[1,94]{1,0:T(1,128)S(1)}, s32[1,94]{1,0:T(1,128)}, u32[]{:S(2)}) copy-start(s32[1,94]{1,0:T(1,128)} %get-tuple-element.325) | copy-start | bytes 1132 | tf_op jit(solution)/shard_map/while
  551.0 83.8 %copy-start.2 = (f32[4,64,128]{2,1,0:T(8,128)S(1)}, f32[4,64,128]{2,1,0:T(8,128)}, u32[]{:S(2)}) copy-start(f32[4,64,128]{2,1,0:T(8,128)} %copy-done.1) | copy-start | bytes 393220 | tf_op jit(solution)/shard_map/while
  627.3 7.5 collective-permute-start
  634.8 96.4 %reduce-scatter.2.cloned.1.call-start = ((), (), s32[]{:S(2)}) async-start(), calls=%async_computation.1 | async-start | bytes 2228224 | tf_op jit(solution)/shard_map/while/body/eval_jaxpr/reduce_scatter | solution.py:39
  636.5 0.7 copy-start.1
  637.9 13.7 %copy-start.4 = (s32[1,94]{1,0:T(1,128)S(1)}, s32[1,94]{1,0:T(1,128)}, u32[]{:S(2)}) copy-start(s32[1,94]{1,0:T(1,128)} %get-tuple-element.325) | copy-start | bytes 1132 | tf_op jit(solution)/shard_map/while
  655.0 83.8 %copy-start.2 = (f32[4,64,128]{2,1,0:T(8,128)S(1)}, f32[4,64,128]{2,1,0:T(8,128)}, u32[]{:S(2)}) copy-start(f32[4,64,128]{2,1,0:T(8,128)} %copy-done.1) | copy-start | bytes 393220 | tf_op jit(solution)/shard_map/while
  731.2 7.5 collective-permute-start
  738.8 96.5 %reduce-scatter.2.cloned.1.call-start = ((), (), s32[]{:S(2)}) async-start(), calls=%async_computation.1 | async-start | bytes 2228224 | tf_op jit(solution)/shard_map/while/body/eval_jaxpr/reduce_scatter | solution.py:39
  740.5 0.7 copy-start.1
  741.9 13.7 %copy-start.4 = (s32[1,94]{1,0:T(1,128)S(1)}, s32[1,94]{1,0:T(1,128)}, u32[]{:S(2)}) copy-start(s32[1,94]{1,0:T(1,128)} %get-tuple-element.325) | copy-start | bytes 1132 | tf_op jit(solution)/shard_map/while
  758.9 83.9 %copy-start.2 = (f32[4,64,128]{2,1,0:T(8,128)S(1)}, f32[4,64,128]{2,1,0:T(8,128)}, u32[]{:S(2)}) copy-start(f32[4,64,128]{2,1,0:T(8,128)} %copy-done.1) | copy-start | bytes 393220 | tf_op jit(solution)/shard_map/while
  835.3 7.6 collective-permute-start
  842.8 0.7 copy-start
  842.8 0.7 copy-start.3
Sparse Core Ops, SparseCore 0:
  30.8 76.8 reduce-scatter.1
  138.0 73.5 reduce-scatter.1
  242.0 73.4 reduce-scatter.1
  345.9 73.4 reduce-scatter.1
  449.8 73.4 reduce-scatter.1
  553.8 73.5 reduce-scatter.1
  657.7 73.5 reduce-scatter.1
  761.6 73.5 reduce-scatter.1
where the time goes:
time: 851 us; the launch traced here: 850 us
  waiting for transfers between devices  609 us (72%)
  matrix products  149 us (18%)
  starting transfers between devices  42.3 us (5%)
  local copies, waits for them, and re-layouts  32.5 us (4%)
  between operations  14 us (2%)
    reduce_scatter x8, waiting for transfers between devices, advance(): lax.psum_scatter(jnp.einsum('kt,ksr->tsr', onehot, products, precision=hi...  593 us
    dot_general x8, matrix products, advance(): products = jnp.einsum('krc,ksc->ksr', factor, picked, precision=highest)  109 us
    ppermute x8, starting transfers between devices, shifted(): return lax.ppermute(block, axis, route)  42.3 us
    dot_general x8, matrix products, advance(): jnp.einsum('kt,ksr->tsr', onehot, products, precision=highest)  26.4 us
    dot_general x8, local copies, waits for them, and re-layouts, advance(): jnp.einsum('kt,ksr->tsr', onehot, products, precision=highest)  20.5 us
  transfers between devices with their start and end apart: 16, of which 16 were waited for; matrix products, arithmetic and copies ran while one was open for 0% of the time, Pallas kernels for 0%

commit v1 on v0

v1 whole, which is shorter than its diff:
```python
import functools

import jax
import jax.numpy as jnp
from jax import lax
from jax.experimental import pallas as pl
from jax.experimental.pallas import tpu as pltpu
from jax.sharding import PartitionSpec as P

BF = jnp.bfloat16
F32 = jnp.float32
VMEM = pl.BlockSpec(memory_space=pltpu.VMEM)
SMEM = pl.BlockSpec(memory_space=pltpu.SMEM)


def split(x):
    high = x.astype(BF)
    return high, (x - high.astype(F32)).astype(BF)


def left_side(x):
    high, low = split(x)
    return jnp.concatenate(
        [
            jnp.concatenate([high, high], 1),
            jnp.concatenate([low, jnp.zeros_like(low)], 1),
        ],
        0,
    )


def product(left, right):
    both = jnp.dot(left, right, preferred_element_type=F32)
    half = both.shape[0] // 2
    return both[:half] + both[half:]


def prepare_body(first, tile_ref, *refs):
    out_ref = refs[-1]

    @pl.loop(0, tile_ref.shape[0], unroll=2)
    def _(i):
        high, low = split(tile_ref[i].T)
        size = high.shape[0]
        out_ref[first + i, :size] = high
        out_ref[first + i, size:] = low


def prepare(tiles, into=None):
    count, size = tiles.shape[0], tiles.shape[1]
    first = 0 if into is None else count
    return pl.pallas_call(
        functools.partial(prepare_body, first),
        out_shape=jax.ShapeDtypeStruct((2 * count, 2 * size, size), BF),
        in_specs=[VMEM] if into is None else [VMEM, VMEM],
        out_specs=VMEM,
        input_output_aliases={} if into is None else {1: 0},
        compiler_params=pltpu.CompilerParams(vmem_limit_bytes=24 << 20),
        name="prepare",
    )(*((tiles,) if into is None else (tiles, into)))


def stage_body(place, rows, cols, arrived, source, inverse, factor, sums, solved, inbound, current):
    slot = place[0]
    live = place[1]
    tiles = factor.shape[0] // 2
    columns = source.shape[0]
    sums[...] = jnp.zeros_like(sums)
    for t in range(columns):
        total = arrived[0, t]
        for j in range(1, arrived.shape[0]):
            total = total + arrived[j, t]
        total = jnp.where(live > 0, total, jnp.zeros_like(total))
        inbound[t] = total
        here = product(left_side(source[t] - total), inverse[slot * columns + t])
        solved[t] = here
        current[t] = left_side(here)
    base = slot * tiles
    for k in range(tiles):
        sums[rows[k]] += product(current[cols[k]], factor[base + k])


def stage(place, rows, cols, arrived, source, inverse, factor, tile_rows):
    columns, width, size = source.shape
    small = jax.ShapeDtypeStruct(source.shape, F32)
    return pl.pallas_call(
        stage_body,
        out_shape=(jax.ShapeDtypeStruct((tile_rows, width, size), F32), small, small),
        in_specs=[SMEM, SMEM, SMEM, VMEM, VMEM, VMEM, VMEM],
        out_specs=[VMEM, VMEM, VMEM],
        scratch_shapes=[pltpu.VMEM((columns, 2 * width, 2 * size), BF)],
        compiler_params=pltpu.CompilerParams(vmem_limit_bytes=6 << 20),
        name="stage",
    )(place, rows, cols, arrived, source, inverse, factor)


def local(sources, diag_inverse, factor_tiles, tile_rows, tile_cols):
    group = lax.axis_index("chain")
    groups = lax.axis_size("chain")
    peers = lax.axis_size("col")
    core = group % 2
    plane = group // 2
    columns = sources.shape[1]
    width = sources.shape[2] // 2

    def swap(x):
        return lax.ppermute(x, "chain", [(i, i ^ 1) for i in range(groups)])

    own_factor = factor_tiles[0]
    other_factor = swap(own_factor)
    own_inverse = diag_inverse[0]
    other_inverse = swap(own_inverse)
    own_rows = tile_rows[0]
    own_cols = tile_cols[0] - lax.axis_index("col") * columns
    own_index = jnp.concatenate([own_rows, own_cols])
    other_index = swap(own_index)
    kept = lax.dynamic_slice_in_dim(sources[0], core * width, width, 1)
    given = lax.dynamic_slice_in_dim(sources[0], (1 - core) * width, width, 1)
    taken = swap(given)

    factor = prepare(other_factor, prepare(own_factor))
    inverse = prepare(other_inverse, prepare(own_inverse))
    count = own_rows.shape[0]
    first = core == 0
    source = [jnp.where(first, kept, taken), jnp.where(first, taken, kept)]
    index = [jnp.where(first, own_index, other_index), jnp.where(first, other_index, own_index)]
    rows = [i[:count] for i in index]
    cols = [i[count:] for i in index]
    slot = [core, 1 - core]
    live = jnp.where(plane > 0, 1, 0)
    place = [jnp.stack([slot[0], live]), jnp.stack([slot[1], jnp.ones_like(live)])]

    def exchange(x):
        return lax.all_to_all(x.reshape((peers, columns) + x.shape[1:]), "col", 0, 0)

    arrived = jnp.zeros((1, columns, width, sources.shape[3]), F32)
    planes = groups // 2
    for sweep in range(planes):
        sums, solved_even, _ = stage(place[0], rows[0], cols[0], arrived, source[0], inverse, factor, peers * columns)
        sums, solved_odd, leaving_even = stage(
            place[1], rows[1], cols[1], exchange(sums), source[1], inverse, factor, peers * columns
        )
        leaving_odd = jnp.sum(exchange(sums), 0)
        if sweep < planes - 1:
            arrived = lax.ppermute(leaving_odd, "chain", [(i, (i + 2) % groups) for i in range(groups)])[None]

    even = jnp.stack([solved_even, leaving_even])
    odd = jnp.stack([solved_odd, leaving_odd])
    mine = jnp.where(first, even, odd)
    partner = swap(jnp.where(first, odd, even))
    whole = jnp.where(first, jnp.concatenate([mine, partner], 2), jnp.concatenate([partner, mine], 2))
    return (whole[0][None], whole[1][None])


def solution(mesh):
    return jax.shard_map(
        local,
        mesh=mesh,
        in_specs=(
            P("chain", "col", None, None),
            P("chain", "col", None, None),
            P("chain", "col", None, None),
            P("chain", "col"),
            P("chain", "col"),
        ),
        out_specs=(P("chain", "col", None, None), P("chain", "col", None, None)),
        check_vma=False,
    )
```

time: 851 us -> 238 us (0.28)
  waiting for transfers between devices: 609 us -> 29.1 us
  matrix products: 149 us -> 0 us
  blocking collectives: 0 us -> 113 us
  Pallas kernels: 0 us -> 32.8 us
  starting transfers between devices: 42.3 us -> 23.4 us
  between operations: 14 us -> 0.82 us
    reduce_scatter x8 -> x0, waiting for transfers between devices: 593 us -> none  [advance(): lax.psum_scatter(jnp.einsum('kt,ksr->tsr', onehot, products, precision=hi...]
    dot_general x24 -> x0, matrix products: 149 us -> none  [the longest x8 109 us: advance(): products = jnp.einsum('krc,ksc->ksr', factor, picked, precision=highest)]
    all_to_all x0 -> x7, blocking collectives: none -> 113 us  [exchange(): lax.all_to_all(x.reshape((peers, columns) + x.shape[1:]), 'col', 0, 0)]
    unnamed x4 -> x22, local copies, waits for them, and re-layouts: 0.7 us -> 34.2 us
    pallas_call x0 -> x12, Pallas kernels: none -> 32.8 us  [the longest x8 19.8 us: stage(): pl.pallas_call(stage_body, out_shape=(jax.ShapeDtypeStruct((tile_rows, wi...]
    ppermute x8, starting transfers between devices: 42.3 us -> 15.7 us  [the longest x5 14 us: swap(): return lax.ppermute(x, 'chain', [(i, i ^ 1) for i in range(groups)])]
    dot_general x8 -> x0, local copies, waits for them, and re-layouts: 20.5 us -> none  [advance(): jnp.einsum('kt,ksr->tsr', onehot, products, precision=highest)]
    all_to_all x0 -> x1, waiting for transfers between devices: none -> 16.1 us  [exchange(): lax.all_to_all(x.reshape((peers, columns) + x.shape[1:]), 'col', 0, 0)]
  transfers between devices with their start and end apart: 16 -> 9, of which waited for: 16 -> 5; matrix products, arithmetic and copies ran while one was open for 0% -> 1% of each run, Pallas kernels for 0% -> 2%
where the time goes in v1:
time: 238 us; the launch traced here: 237 us
  blocking collectives  113 us (47%)
  local copies, waits for them, and re-layouts  35.9 us (15%)
  Pallas kernels  32.8 us (14%)
  waiting for transfers between devices  29.1 us (12%)
  starting transfers between devices  23.4 us (10%)
    all_to_all x7, blocking collectives, exchange(): lax.all_to_all(x.reshape((peers, columns) + x.shape[1:]), 'col', 0, 0)  113 us
    unnamed x22, local copies, waits for them, and re-layouts  34.2 us
    pallas_call x8, Pallas kernels, stage(): pl.pallas_call(stage_body, out_shape=(jax.ShapeDtypeStruct((tile_rows, wi...  19.8 us
    all_to_all x1, waiting for transfers between devices, exchange(): lax.all_to_all(x.reshape((peers, columns) + x.shape[1:]), 'col', 0, 0)  16.1 us
    ppermute x5, starting transfers between devices, swap(): return lax.ppermute(x, 'chain', [(i, i ^ 1) for i in range(groups)])  14 us
    pallas_call x4, Pallas kernels, prepare(): pl.pallas_call(functools.partial(prepare_body, first), out_shape=jax.Shap...  13 us
    ppermute x3, waiting for transfers between devices, local(): lax.ppermute(leaving_odd, 'chain', [(i, (i + 2) % groups) for i in range(...  12 us
    all_to_all x1, starting transfers between devices, exchange(): lax.all_to_all(x.reshape((peers, columns) + x.shape[1:]), 'col', 0, 0)  7.71 us
  transfers between devices with their start and end apart: 9, of which 5 were waited for; matrix products, arithmetic and copies ran while one was open for 1% of the time, Pallas kernels for 2%

profile of v1, /device:TPU:1, one launch (start us, length us, event | category | flops | bytes accessed | tf_op | source)
XLA Modules:
  0.0 237.1 jit_solution(17230752409254586619)
XLA Ops:
  0.7 1.5 collective-permute-start.3
  2.1 0.8 dynamic-slice_bitcast_fusion
  3.0 0.7 subtract_bitcast_fusion
  3.7 0.7 pad_add_fusion
  4.4 0.5 collective-permute-start
  4.9 0.1 pad_add_fusion.1.place
  5.0 2.7 %copy-done.7 = f32[1,94,128,128]{3,2,1,0:T(8,128)S(1)} copy-done((f32[1,94,128,128]{3,2,1,0:T(8,128)S(1)}, f32[1,94,128,128]{3,2,1,0:T(8,128)}, u32[]{:S(2)}) %copy-start.7) | copy-done | bytes 6160408
  7.7 4.9 %prepare.6.refs_0_ = bf16[188,256,128]{2,1,0:T(8,128)(2,1)S(1)} custom-call(f32[94,128,128]{2,1,0:T(8,128)S(1)} %bitcast.29), custom_call_target="tpu_custom_call" | custom-call | tf_op jit(solution)/shard_map/prepare/pallas_call | solution.py:52
  12.7 4.4 %copy-done = bf16[188,256,128]{2,1,0:T(8,128)(2,1)} copy-done((bf16[188,256,128]{2,1,0:T(8,128)(2,1)}, bf16[188,256,128]{2,1,0:T(8,128)(2,1)S(1)}, u32[]{:S(2)}) %copy-start) | copy-done | bytes 12320792
  17.1 0.2 prepare.4.refs_0_
  17.4 0.1 broadcast_select_fusion.1
  17.4 0.1 fusion.3
  17.5 0.2 prepare.5.inverse
  17.8 4.5 %copy-done.1 = bf16[188,256,128]{2,1,0:T(8,128)(2,1)S(1)} copy-done((bf16[188,256,128]{2,1,0:T(8,128)(2,1)S(1)}, bf16[188,256,128]{2,1,0:T(8,128)(2,1)}, u32[]{:S(2)}) %copy-start.1) | copy-done | bytes 12320792
  22.3 7.7 %prepare.7.factor = bf16[188,256,128]{2,1,0:T(8,128)(2,1)S(1)} custom-call(f32[94,128,128]{2,1,0:T(8,128)} %collective-permute-done.3.tile_ref, bf16[188,256,128]{2,1,0:T(8,128)(2,1)S(1)} %copy-done.1), custom_call_target="tpu_custom_call", output_to_operand_aliasing={{}: (1, {})} | custom-call | tf_op jit(solution)/shard_map/prepare/pallas_call | solution.py:52
  30.0 3.0 %stage.8 = (f32[64,32,128]{2,1,0:T(8,128)}, f32[4,32,128]{2,1,0:T(8,128)}, f32[4,32,128]{2,1,0:T(8,128)}) custom-call(s32[2]{0:T(128)S(1)} %pad_add_fusion.1.place, s32[94]{0:T(128)S(1)} %get-tuple-element.33.rows, s32[94]{0:T(128)S(1)} %get-tuple-element.32.cols, f32[1,4,32,128]{3,2,1,0:T(8,128)S(1)} %broadcast_in_dim.12.arrived, ...), custom_call_target="tpu_custom_call" | custom-call | tf_op jit(solution)/shard_map/stage/pallas_call | solution.py:86
  32.9 4.5 %copy-done.2 = bf16[188,256,128]{2,1,0:T(8,128)(2,1)} copy-done((bf16[188,256,128]{2,1,0:T(8,128)(2,1)}, bf16[188,256,128]{2,1,0:T(8,128)(2,1)S(1)}, u32[]{:S(2)}) %copy-start.2) | copy-done | bytes 12320792
  37.4 7.7 %all-to-all-start = ((f32[16,4,32,128]{3,2,1,0:T(8,128)}), f32[16,4,32,128]{3,2,1,0:T(8,128)S(1)}, u32[]{:S(2)}, u32[]{:S(2)}) async-start(f32[16,4,32,128]{3,2,1,0:T(8,128)} %bitcast.9), calls=%async_computation | async-start | bytes 2097152 | tf_op jit(solution)/shard_map/all_to_all | solution.py:134
  45.1 0.1 pad_add_fusion.2.place
  45.2 0.1 fusion.4
  45.2 16.1 %all-to-all-done.arrived = f32[16,4,32,128]{3,2,1,0:T(8,128)S(1)} async-done(((f32[16,4,32,128]{3,2,1,0:T(8,128)}), f32[16,4,32,128]{3,2,1,0:T(8,128)S(1)}, u32[]{:S(2)}, u32[]{:S(2)}) %all-to-all-start) | async-done | bytes 1048608 | tf_op jit(solution)/shard_map/all_to_all | solution.py:134
  61.3 4.5 %copy-done.3 = bf16[188,256,128]{2,1,0:T(8,128)(2,1)S(1)} copy-done((bf16[188,256,128]{2,1,0:T(8,128)(2,1)S(1)}, bf16[188,256,128]{2,1,0:T(8,128)(2,1)}, u32[]{:S(2)}) %copy-start.3) | copy-done | bytes 12320792
  65.8 2.5 %stage.9 = (f32[64,32,128]{2,1,0:T(8,128)S(1)}, f32[4,32,128]{2,1,0:T(8,128)}, f32[4,32,128]{2,1,0:T(8,128)}) custom-call(s32[2]{0:T(128)S(1)} %pad_add_fusion.2.place, s32[94]{0:T(128)S(1)} %get-tuple-element.35.rows, s32[94]{0:T(128)S(1)} %get-tuple-element.34.cols, f32[16,4,32,128]{3,2,1,0:T(8,128)S(1)} %all-to-all-done.arrived, ...), custom_call_target="tpu_custom_call" | custom-call | tf_op jit(solution)/shard_map/stage/pallas_call | solution.py:86
  68.3 20.5 %all_to_all.40 = f32[16,4,32,128]{3,2,1,0:T(8,128)S(1)} all-to-all(f32[16,4,32,128]{3,2,1,0:T(8,128)S(1)} %bitcast.32), channel_id=1, replica_groups=mesh['chain'=8,'col'=16] {'col'}, dimensions={0} | all-to-all | bytes 2097152 | tf_op jit(solution)/shard_map/all_to_all | solution.py:134
  88.9 1.4 collective-permute-start.4
  90.3 3.1 %collective-permute-done.4 = f32[4,32,128]{2,1,0:T(8,128)S(1)} collective-permute-done((f32[4,32,128]{2,1,0:T(8,128)S(1)}, f32[4,32,128]{2,1,0:T(8,128)S(1)}, u32[]{:S(2)}, u32[]{:S(2)}) %collective-permute-start.4) | collective-permute-done | bytes 65568 | tf_op jit(solution)/shard_map/ppermute | solution.py:145
  93.4 4.5 %copy-done.4 = bf16[188,256,128]{2,1,0:T(8,128)(2,1)S(1)} copy-done((bf16[188,256,128]{2,1,0:T(8,128)(2,1)S(1)}, bf16[188,256,128]{2,1,0:T(8,128)(2,1)}, u32[]{:S(2)}) %copy-start.4) | copy-done | bytes 12320792
  97.9 2.5 %stage.10 = (f32[64,32,128]{2,1,0:T(8,128)S(1)}, f32[4,32,128]{2,1,0:T(8,128)}, f32[4,32,128]{2,1,0:T(8,128)}) custom-call(s32[2]{0:T(128)S(1)} %pad_add_fusion.1.place, s32[94]{0:T(128)S(1)} %get-tuple-element.33.rows, s32[94]{0:T(128)S(1)} %get-tuple-element.32.cols, f32[1,4,32,128]{3,2,1,0:T(8,128)S(1)} %bitcast.40, ...), custom_call_target="tpu_custom_call" | custom-call | tf_op jit(solution)/shard_map/stage/pallas_call | solution.py:86
  100.4 18.0 %all_to_all.41.arrived = f32[16,4,32,128]{3,2,1,0:T(8,128)S(1)} all-to-all(f32[16,4,32,128]{3,2,1,0:T(8,128)S(1)} %bitcast.33), channel_id=1, replica_groups=mesh['chain'=8,'col'=16] {'col'}, dimensions={0} | all-to-all | bytes 2097152 | tf_op jit(solution)/shard_map/all_to_all | solution.py:134
  118.4 2.5 %stage.11 = (f32[64,32,128]{2,1,0:T(8,128)S(1)}, f32[4,32,128]{2,1,0:T(8,128)}, f32[4,32,128]{2,1,0:T(8,128)}) custom-call(s32[2]{0:T(128)S(1)} %pad_add_fusion.2.place, s32[94]{0:T(128)S(1)} %get-tuple-element.35.rows, s32[94]{0:T(128)S(1)} %get-tuple-element.34.cols, f32[16,4,32,128]{3,2,1,0:T(8,128)S(1)} %all_to_all.41.arrived, ...), custom_call_target="tpu_custom_call" | custom-call | tf_op jit(solution)/shard_map/stage/pallas_call | solution.py:86
  120.9 16.0 %all_to_all.42 = f32[16,4,32,128]{3,2,1,0:T(8,128)S(1)} all-to-all(f32[16,4,32,128]{3,2,1,0:T(8,128)S(1)} %bitcast.34), channel_id=1, replica_groups=mesh['chain'=8,'col'=16] {'col'}, dimensions={0} | all-to-all | bytes 2097152 | tf_op jit(solution)/shard_map/all_to_all | solution.py:134
  137.0 0.1 collective-permute-start.5
  137.1 4.3 %collective-permute-done.5 = f32[4,32,128]{2,1,0:T(8,128)S(1)} collective-permute-done((f32[4,32,128]{2,1,0:T(8,128)S(1)}, f32[4,32,128]{2,1,0:T(8,128)S(1)}, u32[]{:S(2)}, u32[]{:S(2)}) %collective-permute-start.5) | collective-permute-done | bytes 65568 | tf_op jit(solution)/shard_map/ppermute | solution.py:145
  141.4 4.5 %copy-done.5 = bf16[188,256,128]{2,1,0:T(8,128)(2,1)S(1)} copy-done((bf16[188,256,128]{2,1,0:T(8,128)(2,1)S(1)}, bf16[188,256,128]{2,1,0:T(8,128)(2,1)}, u32[]{:S(2)}) %copy-start.5) | copy-done | bytes 12320792
  145.9 2.5 %stage.12 = (f32[64,32,128]{2,1,0:T(8,128)S(1)}, f32[4,32,128]{2,1,0:T(8,128)}, f32[4,32,128]{2,1,0:T(8,128)}) custom-call(s32[2]{0:T(128)S(1)} %pad_add_fusion.1.place, s32[94]{0:T(128)S(1)} %get-tuple-element.33.rows, s32[94]{0:T(128)S(1)} %get-tuple-element.32.cols, f32[1,4,32,128]{3,2,1,0:T(8,128)S(1)} %bitcast.41, ...), custom_call_target="tpu_custom_call" | custom-call | tf_op jit(solution)/shard_map/stage/pallas_call | solution.py:86
  148.3 15.1 %all_to_all.43.arrived = f32[16,4,32,128]{3,2,1,0:T(8,128)S(1)} all-to-all(f32[16,4,32,128]{3,2,1,0:T(8,128)S(1)} %bitcast.35), channel_id=1, replica_groups=mesh['chain'=8,'col'=16] {'col'}, dimensions={0} | all-to-all | bytes 2097152 | tf_op jit(solution)/shard_map/all_to_all | solution.py:134
  163.4 2.5 %stage.13 = (f32[64,32,128]{2,1,0:T(8,128)S(1)}, f32[4,32,128]{2,1,0:T(8,128)}, f32[4,32,128]{2,1,0:T(8,128)}) custom-call(s32[2]{0:T(128)S(1)} %pad_add_fusion.2.place, s32[94]{0:T(128)S(1)} %get-tuple-element.35.rows, s32[94]{0:T(128)S(1)} %get-tuple-element.34.cols, f32[16,4,32,128]{3,2,1,0:T(8,128)S(1)} %all_to_all.43.arrived, ...), custom_call_target="tpu_custom_call" | custom-call | tf_op jit(solution)/shard_map/stage/pallas_call | solution.py:86
  166.0 14.5 %all_to_all.44 = f32[16,4,32,128]{3,2,1,0:T(8,128)S(1)} all-to-all(f32[16,4,32,128]{3,2,1,0:T(8,128)S(1)} %bitcast.36), channel_id=1, replica_groups=mesh['chain'=8,'col'=16] {'col'}, dimensions={0} | all-to-all | bytes 2097152 | tf_op jit(solution)/shard_map/all_to_all | solution.py:134
  180.5 0.3 collective-permute-start.6
  180.8 4.6 %collective-permute-done.6 = f32[4,32,128]{2,1,0:T(8,128)S(1)} collective-permute-done((f32[4,32,128]{2,1,0:T(8,128)S(1)}, f32[4,32,128]{2,1,0:T(8,128)S(1)}, u32[]{:S(2)}, u32[]{:S(2)}) %collective-permute-start.6) | collective-permute-done | bytes 65568 | tf_op jit(solution)/shard_map/ppermute | solution.py:145
  185.4 4.5 %copy-done.6 = bf16[188,256,128]{2,1,0:T(8,128)(2,1)S(1)} copy-done((bf16[188,256,128]{2,1,0:T(8,128)(2,1)S(1)}, bf16[188,256,128]{2,1,0:T(8,128)(2,1)}, u32[]{:S(2)}) %copy-start.6) | copy-done | bytes 12320792
  189.9 2.4 %stage.14 = (f32[64,32,128]{2,1,0:T(8,128)S(1)}, f32[4,32,128]{2,1,0:T(8,128)S(1)}, f32[4,32,128]{2,1,0:T(8,128)}) custom-call(s32[2]{0:T(128)S(1)} %pad_add_fusion.1.place, s32[94]{0:T(128)S(1)} %get-tuple-element.33.rows, s32[94]{0:T(128)S(1)} %get-tuple-element.32.cols, f32[1,4,32,128]{3,2,1,0:T(8,128)S(1)} %bitcast.39, ...), custom_call_target="tpu_custom_call" | custom-call | tf_op jit(solution)/shard_map/stage/pallas_call | solution.py:86
  192.3 14.5 %all_to_all.45.arrived = f32[16,4,32,128]{3,2,1,0:T(8,128)S(1)} all-to-all(f32[16,4,32,128]{3,2,1,0:T(8,128)S(1)} %bitcast.31), channel_id=1, replica_groups=mesh['chain'=8,'col'=16] {'col'}, dimensions={0} | all-to-all | bytes 2097152 | tf_op jit(solution)/shard_map/all_to_all | solution.py:134
  206.8 2.0 stage.15
  208.7 14.5 %all_to_all.46 = f32[16,4,32,128]{3,2,1,0:T(8,128)S(1)} all-to-all(f32[16,4,32,128]{3,2,1,0:T(8,128)S(1)} %bitcast.30), channel_id=1, replica_groups=mesh['chain'=8,'col'=16] {'col'}, dimensions={0} | all-to-all | bytes 2097152 | tf_op jit(solution)/shard_map/all_to_all | solution.py:134
  223.3 12.0 %collective-permute-start.7 = (f32[2,4,32,128]{3,2,1,0:T(8,128)S(1)}, f32[2,4,32,128]{3,2,1,0:T(8,128)S(1)}, u32[]{:S(2)}, u32[]{:S(2)}) collective-permute-start(f32[2,4,32,128]{3,2,1,0:T(8,128)S(1)} %get-tuple-element.27), channel_id=1, source_target_pairs={{0,16},{16,0},{32,48},{48,32},{64,80},{80,64},{96,112},{112,96},{1... | collective-permute-start | bytes 393224 | tf_op jit(solution)/shard_map/ppermute | solution.py:107
  235.3 1.0 collective-permute-done.7
  236.3 0.7 fusion.2
  (28 shorter events, 0.5 us)
Async XLA Ops:
  0.6 16.9 %copy-start.9 = (f32[1,4,64,128]{3,2,1,0:T(8,128)S(1)}, f32[1,4,64,128]{3,2,1,0:T(8,128)}, u32[]{:S(2)}) copy-start(f32[1,4,64,128]{3,2,1,0:T(8,128)} %param.5) | copy-start | bytes 393220
  0.6 16.7 %copy-start.10 = (s32[1,94]{1,0:T(1,128)S(1)}, s32[1,94]{1,0:T(1,128)}, u32[]{:S(2)}) copy-start(s32[1,94]{1,0:T(1,128)} %param.8) | copy-start | bytes 1132
  0.7 17.1 %collective-permute-start.3 = (f32[94,128,128]{2,1,0:T(8,128)}, f32[94,128,128]{2,1,0:T(8,128)}, u32[]{:S(2)}, u32[]{:S(2)}) collective-permute-start(f32[94,128,128]{2,1,0:T(8,128)} %bitcast.28), channel_id=1, source_target_pairs={{0,16},{16,0},{32,48},{48,32},{64,80},{80,64},{96,112},{112,96},{1... | collective-permute-start | bytes 18481160 | tf_op jit(solution)/shard_map/ppermute | solution.py:107
  3.0 14.5 %collective-permute-start.1 = (f32[4,32,128]{2,1,0:T(8,128)S(1)}, f32[4,32,128]{2,1,0:T(8,128)S(1)}, u32[]{:S(2)}, u32[]{:S(2)}) collective-permute-start(f32[4,32,128]{2,1,0:T(8,128)S(1)} %dynamic-slice_bitcast_fusion), channel_id=1, source_target_pairs={{0,16},{16,0},{32,48},{48,32},{64,80},{80,64},{96,112},{112,96},{1... | collective-permute-start | bytes 196616 | tf_op jit(solution)/shard_map/ppermute | solution.py:107
  4.4 12.9 %collective-permute-start = (s32[188]{0:T(256)S(1)}, s32[188]{0:T(256)S(1)}, u32[]{:S(2)}, u32[]{:S(2)}) collective-permute-start(s32[188]{0:T(256)S(1)} %pad_add_fusion), channel_id=1, source_target_pairs={{0,16},{16,0},{32,48},{48,32},{64,80},{80,64},{96,112},{112,96},{1... | collective-permute-start | bytes 2264 | tf_op jit(solution)/shard_map/ppermute | solution.py:107
  4.9 12.7 %collective-permute-start.2 = (f32[4,128,128]{2,1,0:T(8,128)}, f32[4,128,128]{2,1,0:T(8,128)S(1)}, u32[]{:S(2)}, u32[]{:S(2)}) collective-permute-start(f32[4,128,128]{2,1,0:T(8,128)} %bitcast.37), channel_id=1, source_target_pairs={{0,16},{16,0},{32,48},{48,32},{64,80},{80,64},{96,112},{112,96},{1... | collective-permute-start | bytes 786440 | tf_op jit(solution)/shard_map/ppermute | solution.py:107
  5.0 2.7 %copy-start.7 = (f32[1,94,128,128]{3,2,1,0:T(8,128)S(1)}, f32[1,94,128,128]{3,2,1,0:T(8,128)}, u32[]{:S(2)}) copy-start(f32[1,94,128,128]{3,2,1,0:T(8,128)} %param.7) | copy-start | bytes 18481156
  7.7 9.4 %copy-start.8 = (f32[1,4,128,128]{3,2,1,0:T(8,128)S(1)}, f32[1,4,128,128]{3,2,1,0:T(8,128)}, u32[]{:S(2)}) copy-start(f32[1,4,128,128]{3,2,1,0:T(8,128)} %param.6) | copy-start | bytes 786436
  12.7 4.5 %copy-start = (bf16[188,256,128]{2,1,0:T(8,128)(2,1)}, bf16[188,256,128]{2,1,0:T(8,128)(2,1)S(1)}, u32[]{:S(2)}) copy-start(bf16[188,256,128]{2,1,0:T(8,128)(2,1)S(1)} %prepare.6.refs_0_) | copy-start | bytes 36962308
  17.8 4.5 %copy-start.1 = (bf16[188,256,128]{2,1,0:T(8,128)(2,1)S(1)}, bf16[188,256,128]{2,1,0:T(8,128)(2,1)}, u32[]{:S(2)}) copy-start(bf16[188,256,128]{2,1,0:T(8,128)(2,1)} %copy-done) | copy-start | bytes 36962308
  32.9 4.5 %copy-start.2 = (bf16[188,256,128]{2,1,0:T(8,128)(2,1)}, bf16[188,256,128]{2,1,0:T(8,128)(2,1)S(1)}, u32[]{:S(2)}) copy-start(bf16[188,256,128]{2,1,0:T(8,128)(2,1)S(1)} %prepare.7.factor) | copy-start | bytes 36962308
  37.4 24.0 %all-to-all-start = ((f32[16,4,32,128]{3,2,1,0:T(8,128)}), f32[16,4,32,128]{3,2,1,0:T(8,128)S(1)}, u32[]{:S(2)}, u32[]{:S(2)}) async-start(f32[16,4,32,128]{3,2,1,0:T(8,128)} %bitcast.9), calls=%async_computation | async-start | bytes 2097152 | tf_op jit(solution)/shard_map/all_to_all | solution.py:134
  61.3 4.5 %copy-start.3 = (bf16[188,256,128]{2,1,0:T(8,128)(2,1)S(1)}, bf16[188,256,128]{2,1,0:T(8,128)(2,1)}, u32[]{:S(2)}) copy-start(bf16[188,256,128]{2,1,0:T(8,128)(2,1)} %copy-done.2) | copy-start | bytes 36962308
  88.9 4.5 %collective-permute-start.4 = (f32[4,32,128]{2,1,0:T(8,128)S(1)}, f32[4,32,128]{2,1,0:T(8,128)S(1)}, u32[]{:S(2)}, u32[]{:S(2)}) collective-permute-start(f32[4,32,128]{2,1,0:T(8,128)S(1)} %reduce_sum.36), channel_id=1, source_target_pairs={{0,32},{16,48},{32,64},{48,80},{64,96},{80,112},{96,0},{112,16},{1... | collective-permute-start | bytes 196616 | tf_op jit(solution)/shard_map/ppermute | solution.py:145
  93.4 4.5 %copy-start.4 = (bf16[188,256,128]{2,1,0:T(8,128)(2,1)S(1)}, bf16[188,256,128]{2,1,0:T(8,128)(2,1)}, u32[]{:S(2)}) copy-start(bf16[188,256,128]{2,1,0:T(8,128)(2,1)} %copy-done.2) | copy-start | bytes 36962308
  137.0 4.4 %collective-permute-start.5 = (f32[4,32,128]{2,1,0:T(8,128)S(1)}, f32[4,32,128]{2,1,0:T(8,128)S(1)}, u32[]{:S(2)}, u32[]{:S(2)}) collective-permute-start(f32[4,32,128]{2,1,0:T(8,128)S(1)} %reduce_sum.37), channel_id=1, source_target_pairs={{0,32},{16,48},{32,64},{48,80},{64,96},{80,112},{96,0},{112,16},{1... | collective-permute-start | bytes 196616 | tf_op jit(solution)/shard_map/ppermute | solution.py:145
  141.4 4.5 %copy-start.5 = (bf16[188,256,128]{2,1,0:T(8,128)(2,1)S(1)}, bf16[188,256,128]{2,1,0:T(8,128)(2,1)}, u32[]{:S(2)}) copy-start(bf16[188,256,128]{2,1,0:T(8,128)(2,1)} %copy-done.2) | copy-start | bytes 36962308
  180.5 4.9 %collective-permute-start.6 = (f32[4,32,128]{2,1,0:T(8,128)S(1)}, f32[4,32,128]{2,1,0:T(8,128)S(1)}, u32[]{:S(2)}, u32[]{:S(2)}) collective-permute-start(f32[4,32,128]{2,1,0:T(8,128)S(1)} %reduce_sum.38), channel_id=1, source_target_pairs={{0,32},{16,48},{32,64},{48,80},{64,96},{80,112},{96,0},{112,16},{1... | collective-permute-start | bytes 196616 | tf_op jit(solution)/shard_map/ppermute | solution.py:145
  185.4 4.5 %copy-start.6 = (bf16[188,256,128]{2,1,0:T(8,128)(2,1)S(1)}, bf16[188,256,128]{2,1,0:T(8,128)(2,1)}, u32[]{:S(2)}) copy-start(bf16[188,256,128]{2,1,0:T(8,128)(2,1)} %copy-done.2) | copy-start | bytes 36962308
  223.3 13.0 %collective-permute-start.7 = (f32[2,4,32,128]{3,2,1,0:T(8,128)S(1)}, f32[2,4,32,128]{3,2,1,0:T(8,128)S(1)}, u32[]{:S(2)}, u32[]{:S(2)}) collective-permute-start(f32[2,4,32,128]{3,2,1,0:T(8,128)S(1)} %get-tuple-element.27), channel_id=1, source_target_pairs={{0,16},{16,0},{32,48},{48,32},{64,80},{80,64},{96,112},{112,96},{1... | collective-permute-start | bytes 393224 | tf_op jit(solution)/shard_map/ppermute | solution.py:107

commit v2 on v1

v2 whole, which is shorter than its diff:
```python
import functools

import jax
import jax.numpy as jnp
from jax import lax
from jax.experimental import pallas as pl
from jax.experimental.pallas import tpu as pltpu
from jax.sharding import PartitionSpec as P

BF = jnp.bfloat16
F32 = jnp.float32
VMEM = pl.BlockSpec(memory_space=pltpu.VMEM)
SMEM = pl.BlockSpec(memory_space=pltpu.SMEM)


def split(x):
    high = x.astype(BF)
    return high, (x - high.astype(F32)).astype(BF)


def left_side(x):
    high, low = split(x)
    return jnp.concatenate(
        [
            jnp.concatenate([high, high], 1),
            jnp.concatenate([low, jnp.zeros_like(low)], 1),
        ],
        0,
    )


def product(left, right):
    both = jnp.dot(left, right, preferred_element_type=F32)
    half = both.shape[0] // 2
    return both[:half] + both[half:]


def prepare_tile(tile, out_ref, at):
    high, low = split(tile.T)
    size = high.shape[0]
    out_ref[at, :size] = high
    out_ref[at, size:] = low


def prepare_body(first, tile_ref, *refs):
    out_ref = refs[-1]

    @pl.loop(0, tile_ref.shape[0], unroll=8)
    def _(i):
        prepare_tile(tile_ref[i], out_ref, first + i)


def prepare(tiles, other_tiles):
    count, size = tiles.shape[0], tiles.shape[1]
    both = jax.ShapeDtypeStruct((2 * count, 2 * size, size), BF)
    grant = pltpu.CompilerParams(vmem_limit_bytes=20 << 20)
    half = pl.pallas_call(
        functools.partial(prepare_body, 0),
        out_shape=both,
        in_specs=[VMEM],
        out_specs=VMEM,
        compiler_params=grant,
        name="prepare_first",
    )(tiles)
    return pl.pallas_call(
        functools.partial(prepare_body, count),
        out_shape=both,
        in_specs=[VMEM, VMEM],
        out_specs=VMEM,
        input_output_aliases={1: 0},
        compiler_params=grant,
        name="prepare_second",
    )(other_tiles, half)


def gather_sum_body(arrived, total):
    for t in range(arrived.shape[1]):
        value = arrived[0, t]
        for j in range(1, arrived.shape[0]):
            value = value + arrived[j, t]
        total[t] = value


def gather_sum(arrived):
    return pl.pallas_call(
        gather_sum_body,
        out_shape=jax.ShapeDtypeStruct(arrived.shape[1:], F32),
        in_specs=[VMEM],
        out_specs=VMEM,
        compiler_params=pltpu.CompilerParams(vmem_limit_bytes=4 << 20),
        name="gather_sum",
    )(arrived)


def stage_body(
    place, rows, cols, other_rows, other_cols, arrived, source, other_source, inverse, factor, sums, solved, inbound, current
):
    slot, live, first, shift = place[0], place[1], place[2], place[3]
    tiles = factor.shape[0] // 2
    columns, width = inbound.shape[0], inbound.shape[1]
    here = pl.ds(pl.multiple_of(first, width), width)
    sums[...] = jnp.zeros_like(sums)
    for t in range(columns):
        total = arrived[0, t]
        for j in range(1, arrived.shape[0]):
            total = total + arrived[j, t]
        total = jnp.where(live > 0, total, jnp.zeros_like(total))
        inbound[t] = total
        right = jnp.where(slot > 0, other_source[0, t, here], source[0, t, here]) - total
        value = product(left_side(right), inverse[slot * columns + t])
        solved[t] = value
        current[t] = left_side(value)
    base = slot * tiles
    for k in range(tiles):
        row = jnp.where(slot > 0, other_rows[0, k], rows[0, k])
        col = jnp.where(slot > 0, other_cols[0, k], cols[0, k]) - shift
        sums[row] += product(current[col], factor[base + k])


def stage(place, tables, arrived, inputs, tile_rows):
    small = jax.ShapeDtypeStruct(arrived.shape[1:], F32)
    columns, width, size = small.shape
    return pl.pallas_call(
        stage_body,
        out_shape=(jax.ShapeDtypeStruct((tile_rows, width, size), F32), small, small),
        in_specs=[SMEM] * 5 + [VMEM] * 5,
        out_specs=[VMEM, VMEM, VMEM],
        scratch_shapes=[pltpu.VMEM((columns, 2 * width, 2 * size), BF)],
        compiler_params=pltpu.CompilerParams(vmem_limit_bytes=6 << 20),
        name="stage",
    )(place, *tables, arrived, *inputs)


def local(sources, diag_inverse, factor_tiles, tile_rows, tile_cols):
    group = lax.axis_index("chain")
    groups = lax.axis_size("chain")
    peers = lax.axis_size("col")
    core = lax.rem(group, 2)
    columns = sources.shape[1]
    width = sources.shape[2] // 2

    def swap(x):
        return lax.ppermute(x, "chain", [(i, i ^ 1) for i in range(groups)])

    def exchange(x):
        return lax.all_to_all(x.reshape((peers, columns) + x.shape[1:]), "col", 0, 0)

    lowest = core * width
    shift = lax.axis_index("col") * columns
    live = jnp.where(group > 1, 1, 0)
    place = [jnp.stack([core, live, lowest, shift]), jnp.stack([1 - core, jnp.ones_like(live), lowest, shift])]
    place, factor_tiles = lax.optimization_barrier((place, factor_tiles))

    other_factor = swap(factor_tiles[0])
    other_inverse = swap(diag_inverse[0])
    tables = (tile_rows, tile_cols, swap(tile_rows), swap(tile_cols))
    inputs = (
        sources,
        swap(sources),
        prepare(diag_inverse[0], other_inverse),
        prepare(factor_tiles[0], other_factor),
    )

    arrived = jnp.zeros((1, columns, width, sources.shape[3]), F32)
    planes = groups // 2
    for sweep in range(planes):
        sums, solved_even, _ = stage(place[0], tables, arrived, inputs, peers * columns)
        sums, solved_odd, leaving_even = stage(place[1], tables, exchange(sums), inputs, peers * columns)
        leaving_odd = gather_sum(exchange(sums))
        if sweep < planes - 1:
            arrived = lax.ppermute(leaving_odd, "chain", [(i, (i + 2) % groups) for i in range(groups)])[None]

    first = core == 0
    even = jnp.stack([solved_even, leaving_even])
    odd = jnp.stack([solved_odd, leaving_odd])
    mine = jnp.where(first, even, odd)
    partner = swap(jnp.where(first, odd, even))
    whole = jnp.where(first, jnp.concatenate([mine, partner], 2), jnp.concatenate([partner, mine], 2))
    return (whole[0][None], whole[1][None])


def solution(mesh):
    return jax.shard_map(
        local,
        mesh=mesh,
        in_specs=(
            P("chain", "col", None, None),
            P("chain", "col", None, None),
            P("chain", "col", None, None),
            P("chain", "col"),
            P("chain", "col"),
        ),
        out_specs=(P("chain", "col", None, None), P("chain", "col", None, None)),
        check_vma=False,
    )
```

time: 238 us -> 200 us (0.84)
  local copies, waits for them, and re-layouts: 35.9 us -> 3.5 us
  blocking collectives: 113 us -> 119 us
  Pallas kernels: 32.8 us -> 27.3 us
  starting transfers between devices: 23.4 us -> 19.6 us
    unnamed x22 -> x10, local copies, waits for them, and re-layouts: 34.2 us -> 2.77 us
    all_to_all x7, blocking collectives: 113 us -> 119 us  [exchange(): lax.all_to_all(x.reshape((peers, columns) + x.shape[1:]), 'col', 0, 0)]
    pallas_call x4 -> x8, Pallas kernels: 13 us -> 6.82 us  [the longest x2 3.3 us: prepare(): pl.pallas_call(functools.partial(prepare_body, count), out_shape=both, in...]
    all_to_all x1, starting transfers between devices: 7.71 us -> 3.65 us  [exchange(): lax.all_to_all(x.reshape((peers, columns) + x.shape[1:]), 'col', 0, 0)]
    all_to_all x1, waiting for transfers between devices: 16.1 us -> 12.1 us  [exchange(): lax.all_to_all(x.reshape((peers, columns) + x.shape[1:]), 'col', 0, 0)]
    ppermute x5 -> x6, waiting for transfers between devices: 1 us -> 4.08 us  [swap(): return lax.ppermute(x, 'chain', [(i, i ^ 1) for i in range(groups)])]
    ppermute x5 -> x6, starting transfers between devices: 14 us -> 14.5 us  [swap(): return lax.ppermute(x, 'chain', [(i, i ^ 1) for i in range(groups)])]
  transfers between devices with their start and end apart: 9 -> 10, of which waited for: 5 -> 6; matrix products, arithmetic and copies ran while one was open for 1% -> 0% of each run, Pallas kernels for 2% -> 3%
where the time goes in v2:
time: 200 us; the launch traced here: 199 us
  blocking collectives  119 us (60%)
  waiting for transfers between devices  28.5 us (14%)
  Pallas kernels  27.3 us (14%)
  starting transfers between devices  19.6 us (10%)
  local copies, waits for them, and re-layouts  3.5 us (2%)
    all_to_all x7, blocking collectives, exchange(): lax.all_to_all(x.reshape((peers, columns) + x.shape[1:]), 'col', 0, 0)  119 us
    pallas_call x8, Pallas kernels, stage(): pl.pallas_call(stage_body, out_shape=(jax.ShapeDtypeStruct((tile_rows, wi...  20.5 us
    ppermute x6, starting transfers between devices, swap(): return lax.ppermute(x, 'chain', [(i, i ^ 1) for i in range(groups)])  14.5 us
    ppermute x3, waiting for transfers between devices, local(): lax.ppermute(leaving_odd, 'chain', [(i, (i + 2) % groups) for i in range(...  12.3 us
    all_to_all x1, waiting for transfers between devices, exchange(): lax.all_to_all(x.reshape((peers, columns) + x.shape[1:]), 'col', 0, 0)  12.1 us
    ppermute x6, waiting for transfers between devices, swap(): return lax.ppermute(x, 'chain', [(i, i ^ 1) for i in range(groups)])  4.08 us
  transfers between devices with their start and end apart: 10, of which 6 were waited for; matrix products, arithmetic and copies ran while one was open for 0% of the time, Pallas kernels for 3%

profile of v2, /device:TPU:1, one launch (start us, length us, event | category | flops | bytes accessed | tf_op | source)
XLA Modules:
  0.0 199.3 jit_solution(2101767486123653543)
XLA Ops:
  0.6 0.1 add_add_fusion
  0.7 1.4 collective-permute-start.4
  2.1 0.1 collective-permute-start.3
  2.2 0.4 collective-permute-start.2
  2.6 0.1 collective-permute-start
  2.7 0.4 collective-permute-start.1
  3.1 2.7 %copy-done.1 = f32[1,94,128,128]{3,2,1,0:T(8,128)S(1)} copy-done((f32[1,94,128,128]{3,2,1,0:T(8,128)S(1)}, f32[1,94,128,128]{3,2,1,0:T(8,128)}, u32[]{:S(2)}) %copy-start.1) | copy-done | bytes 6160408
  5.9 2.9 %prepare_first.3.refs_0_ = bf16[188,256,128]{2,1,0:T(8,128)(2,1)S(1)} custom-call(f32[94,128,128]{2,1,0:T(8,128)S(1)} %bitcast.23), custom_call_target="tpu_custom_call" | custom-call | tf_op jit(solution)/shard_map/prepare_first/pallas_call | solution.py:57
  8.8 0.4 prepare_first.2.refs_0_
  9.2 3.1 %collective-permute-done.3.tile_ref = f32[4,128,128]{2,1,0:T(8,128)S(1)} collective-permute-done((f32[4,128,128]{2,1,0:T(8,128)}, f32[4,128,128]{2,1,0:T(8,128)S(1)}, u32[]{:S(2)}, u32[]{:S(2)}) %collective-permute-start.3) | collective-permute-done | bytes 262176 | tf_op jit(solution)/shard_map/ppermute | solution.py:143
  12.3 0.4 prepare_second.2.inverse
  12.7 0.0 copy-start
  12.7 0.0 copy-start.3
  12.7 0.0 copy-start.4
  12.8 0.0 collective-permute-done.4.tile_ref
  12.8 2.9 %prepare_second.3.factor = bf16[188,256,128]{2,1,0:T(8,128)(2,1)S(1)} custom-call(f32[94,128,128]{2,1,0:T(8,128)S(1)} %collective-permute-done.4.tile_ref, bf16[188,256,128]{2,1,0:T(8,128)(2,1)S(1)} %prepare_first.3.refs_0_), custom_call_target="tpu_custom_call", output_to_operand_aliasing={{}: (1, {})} | custom-call | tf_op jit(solution)/shard_map/prepare_second/pallas_call | solution.py:65
  15.7 0.0 collective-permute-done.1.other_cols
  15.7 0.0 collective-permute-done.2.other_source
  15.7 2.5 %stage.8 = (f32[64,32,128]{2,1,0:T(8,128)S(1)}, f32[4,32,128]{2,1,0:T(8,128)}, f32[4,32,128]{2,1,0:T(8,128)}) custom-call(s32[4]{0:T(128)S(1)} %get-tuple-element.16.place, s32[1,94]{1,0:T(1,128)S(1)} %copy-done.3, s32[1,94]{1,0:T(1,128)S(1)} %copy-done.4, s32[1,94]{1,0:T(1,128)S(1)} %collective-permute-done.other_rows, ...), custom_call_target="tpu_custom_call" | custom-call | tf_op jit(solution)/shard_map/stage/pallas_call | solution.py:123
  18.3 23.8 %all_to_all.40.arrived = f32[16,4,32,128]{3,2,1,0:T(8,128)S(1)} all-to-all(f32[16,4,32,128]{3,2,1,0:T(8,128)S(1)} %bitcast.25), channel_id=1, replica_groups=mesh['chain'=8,'col'=16] {'col'}, dimensions={0} | all-to-all | bytes 2097152 | tf_op jit(solution)/shard_map/all_to_all | solution.py:146
  42.1 2.5 %stage.9 = (f32[64,32,128]{2,1,0:T(8,128)S(1)}, f32[4,32,128]{2,1,0:T(8,128)}, f32[4,32,128]{2,1,0:T(8,128)}) custom-call(s32[4]{0:T(128)S(1)} %get-tuple-element.17.place, s32[1,94]{1,0:T(1,128)S(1)} %copy-done.3, s32[1,94]{1,0:T(1,128)S(1)} %copy-done.4, s32[1,94]{1,0:T(1,128)S(1)} %collective-permute-done.other_rows, ...), custom_call_target="tpu_custom_call" | custom-call | tf_op jit(solution)/shard_map/stage/pallas_call | solution.py:123
  44.6 19.1 %all_to_all.41.arrived = f32[16,4,32,128]{3,2,1,0:T(8,128)S(1)} all-to-all(f32[16,4,32,128]{3,2,1,0:T(8,128)S(1)} %bitcast.26), channel_id=1, replica_groups=mesh['chain'=8,'col'=16] {'col'}, dimensions={0} | all-to-all | bytes 2097152 | tf_op jit(solution)/shard_map/all_to_all | solution.py:146
  63.7 0.1 gather_sum.4
  63.8 1.4 collective-permute-start.5
  65.1 3.1 %collective-permute-done.5 = f32[4,32,128]{2,1,0:T(8,128)S(1)} collective-permute-done((f32[4,32,128]{2,1,0:T(8,128)S(1)}, f32[4,32,128]{2,1,0:T(8,128)S(1)}, u32[]{:S(2)}, u32[]{:S(2)}) %collective-permute-start.5) | collective-permute-done | bytes 65568 | tf_op jit(solution)/shard_map/ppermute | solution.py:171
  68.2 2.5 %stage.10 = (f32[64,32,128]{2,1,0:T(8,128)S(1)}, f32[4,32,128]{2,1,0:T(8,128)}, f32[4,32,128]{2,1,0:T(8,128)}) custom-call(s32[4]{0:T(128)S(1)} %get-tuple-element.16.place, s32[1,94]{1,0:T(1,128)S(1)} %copy-done.3, s32[1,94]{1,0:T(1,128)S(1)} %copy-done.4, s32[1,94]{1,0:T(1,128)S(1)} %collective-permute-done.other_rows, ...), custom_call_target="tpu_custom_call" | custom-call | tf_op jit(solution)/shard_map/stage/pallas_call | solution.py:123
  70.8 16.7 %all_to_all.42.arrived = f32[16,4,32,128]{3,2,1,0:T(8,128)S(1)} all-to-all(f32[16,4,32,128]{3,2,1,0:T(8,128)S(1)} %bitcast.27), channel_id=1, replica_groups=mesh['chain'=8,'col'=16] {'col'}, dimensions={0} | all-to-all | bytes 2097152 | tf_op jit(solution)/shard_map/all_to_all | solution.py:146
  87.5 2.5 %stage.11 = (f32[64,32,128]{2,1,0:T(8,128)S(1)}, f32[4,32,128]{2,1,0:T(8,128)}, f32[4,32,128]{2,1,0:T(8,128)}) custom-call(s32[4]{0:T(128)S(1)} %get-tuple-element.17.place, s32[1,94]{1,0:T(1,128)S(1)} %copy-done.3, s32[1,94]{1,0:T(1,128)S(1)} %copy-done.4, s32[1,94]{1,0:T(1,128)S(1)} %collective-permute-done.other_rows, ...), custom_call_target="tpu_custom_call" | custom-call | tf_op jit(solution)/shard_map/stage/pallas_call | solution.py:123
  90.0 16.1 %all_to_all.43.arrived = f32[16,4,32,128]{3,2,1,0:T(8,128)S(1)} all-to-all(f32[16,4,32,128]{3,2,1,0:T(8,128)S(1)} %bitcast.28), channel_id=1, replica_groups=mesh['chain'=8,'col'=16] {'col'}, dimensions={0} | all-to-all | bytes 2097152 | tf_op jit(solution)/shard_map/all_to_all | solution.py:146
  106.1 0.1 gather_sum.5
  106.1 0.1 collective-permute-start.6
  106.2 4.6 %collective-permute-done.6 = f32[4,32,128]{2,1,0:T(8,128)S(1)} collective-permute-done((f32[4,32,128]{2,1,0:T(8,128)S(1)}, f32[4,32,128]{2,1,0:T(8,128)S(1)}, u32[]{:S(2)}, u32[]{:S(2)}) %collective-permute-start.6) | collective-permute-done | bytes 65568 | tf_op jit(solution)/shard_map/ppermute | solution.py:171
  110.8 2.5 %stage.12 = (f32[64,32,128]{2,1,0:T(8,128)S(1)}, f32[4,32,128]{2,1,0:T(8,128)}, f32[4,32,128]{2,1,0:T(8,128)}) custom-call(s32[4]{0:T(128)S(1)} %get-tuple-element.16.place, s32[1,94]{1,0:T(1,128)S(1)} %copy-done.3, s32[1,94]{1,0:T(1,128)S(1)} %copy-done.4, s32[1,94]{1,0:T(1,128)S(1)} %collective-permute-done.other_rows, ...), custom_call_target="tpu_custom_call" | custom-call | tf_op jit(solution)/shard_map/stage/pallas_call | solution.py:123
  113.3 14.5 %all_to_all.44.arrived = f32[16,4,32,128]{3,2,1,0:T(8,128)S(1)} all-to-all(f32[16,4,32,128]{3,2,1,0:T(8,128)S(1)} %bitcast.29), channel_id=1, replica_groups=mesh['chain'=8,'col'=16] {'col'}, dimensions={0} | all-to-all | bytes 2097152 | tf_op jit(solution)/shard_map/all_to_all | solution.py:146
  127.8 2.5 %stage.13 = (f32[64,32,128]{2,1,0:T(8,128)S(1)}, f32[4,32,128]{2,1,0:T(8,128)}, f32[4,32,128]{2,1,0:T(8,128)}) custom-call(s32[4]{0:T(128)S(1)} %get-tuple-element.17.place, s32[1,94]{1,0:T(1,128)S(1)} %copy-done.3, s32[1,94]{1,0:T(1,128)S(1)} %copy-done.4, s32[1,94]{1,0:T(1,128)S(1)} %collective-permute-done.other_rows, ...), custom_call_target="tpu_custom_call" | custom-call | tf_op jit(solution)/shard_map/stage/pallas_call | solution.py:123
  130.4 14.7 %all_to_all.45.arrived = f32[16,4,32,128]{3,2,1,0:T(8,128)S(1)} all-to-all(f32[16,4,32,128]{3,2,1,0:T(8,128)S(1)} %bitcast.30), channel_id=1, replica_groups=mesh['chain'=8,'col'=16] {'col'}, dimensions={0} | all-to-all | bytes 2097152 | tf_op jit(solution)/shard_map/all_to_all | solution.py:146
  145.0 0.1 gather_sum.6
  145.1 0.1 collective-permute-start.7
  145.1 4.6 %collective-permute-done.7 = f32[4,32,128]{2,1,0:T(8,128)S(1)} collective-permute-done((f32[4,32,128]{2,1,0:T(8,128)S(1)}, f32[4,32,128]{2,1,0:T(8,128)S(1)}, u32[]{:S(2)}, u32[]{:S(2)}) %collective-permute-start.7) | collective-permute-done | bytes 65568 | tf_op jit(solution)/shard_map/ppermute | solution.py:171
  149.8 2.5 %stage.14 = (f32[64,32,128]{2,1,0:T(8,128)S(1)}, f32[4,32,128]{2,1,0:T(8,128)S(1)}, f32[4,32,128]{2,1,0:T(8,128)}) custom-call(s32[4]{0:T(128)S(1)} %get-tuple-element.16.place, s32[1,94]{1,0:T(1,128)S(1)} %copy-done.3, s32[1,94]{1,0:T(1,128)S(1)} %copy-done.4, s32[1,94]{1,0:T(1,128)S(1)} %collective-permute-done.other_rows, ...), custom_call_target="tpu_custom_call" | custom-call | tf_op jit(solution)/shard_map/stage/pallas_call | solution.py:123
  152.2 14.5 %all_to_all.46.arrived = f32[16,4,32,128]{3,2,1,0:T(8,128)S(1)} all-to-all(f32[16,4,32,128]{3,2,1,0:T(8,128)S(1)} %bitcast.24), channel_id=1, replica_groups=mesh['chain'=8,'col'=16] {'col'}, dimensions={0} | all-to-all | bytes 2097152 | tf_op jit(solution)/shard_map/all_to_all | solution.py:146
  166.7 3.0 %stage.15 = (f32[64,32,128]{2,1,0:T(8,128)}, f32[4,32,128]{2,1,0:T(8,128)S(1)}, f32[4,32,128]{2,1,0:T(8,128)S(1)}) custom-call(s32[4]{0:T(128)S(1)} %get-tuple-element.17.place, s32[1,94]{1,0:T(1,128)S(1)} %copy-done.3, s32[1,94]{1,0:T(1,128)S(1)} %copy-done.4, s32[1,94]{1,0:T(1,128)S(1)} %collective-permute-done.other_rows, ...), custom_call_target="tpu_custom_call" | custom-call | tf_op jit(solution)/shard_map/stage/pallas_call | solution.py:123
  169.7 3.7 %all-to-all-start.7 = ((f32[16,4,32,128]{3,2,1,0:T(8,128)}), f32[16,4,32,128]{3,2,1,0:T(8,128)S(1)}, u32[]{:S(2)}, u32[]{:S(2)}) async-start(f32[16,4,32,128]{3,2,1,0:T(8,128)} %bitcast.20), calls=%async_computation.7 | async-start | bytes 2097152 | tf_op jit(solution)/shard_map/all_to_all | solution.py:146
  173.3 12.1 %all-to-all-done.7.arrived = f32[16,4,32,128]{3,2,1,0:T(8,128)S(1)} async-done(((f32[16,4,32,128]{3,2,1,0:T(8,128)}), f32[16,4,32,128]{3,2,1,0:T(8,128)S(1)}, u32[]{:S(2)}, u32[]{:S(2)}) %all-to-all-start.7) | async-done | bytes 1048608 | tf_op jit(solution)/shard_map/all_to_all | solution.py:146
  185.5 0.1 gather_sum.7
  185.6 12.0 %collective-permute-start.8 = (f32[2,4,32,128]{3,2,1,0:T(8,128)S(1)}, f32[2,4,32,128]{3,2,1,0:T(8,128)S(1)}, u32[]{:S(2)}, u32[]{:S(2)}) collective-permute-start(f32[2,4,32,128]{3,2,1,0:T(8,128)S(1)} %get-tuple-element.33), channel_id=1, source_target_pairs={{0,16},{16,0},{32,48},{48,32},{64,80},{80,64},{96,112},{112,96},{1... | collective-permute-start | bytes 393224 | tf_op jit(solution)/shard_map/ppermute | solution.py:143
  197.6 1.0 collective-permute-done.8
  198.6 0.7 fusion.2
  (10 shorter events, 0.1 us)
Async XLA Ops:
  0.7 12.0 %collective-permute-start.4 = (f32[94,128,128]{2,1,0:T(8,128)}, f32[94,128,128]{2,1,0:T(8,128)S(1)}, u32[]{:S(2)}, u32[]{:S(2)}) collective-permute-start(f32[94,128,128]{2,1,0:T(8,128)} %bitcast.22), channel_id=1, source_target_pairs={{0,16},{16,0},{32,48},{48,32},{64,80},{80,64},{96,112},{112,96},{1... | collective-permute-start | bytes 18481160 | tf_op jit(solution)/shard_map/ppermute | solution.py:143
  2.1 10.2 %collective-permute-start.3 = (f32[4,128,128]{2,1,0:T(8,128)}, f32[4,128,128]{2,1,0:T(8,128)S(1)}, u32[]{:S(2)}, u32[]{:S(2)}) collective-permute-start(f32[4,128,128]{2,1,0:T(8,128)} %bitcast.31), channel_id=1, source_target_pairs={{0,16},{16,0},{32,48},{48,32},{64,80},{80,64},{96,112},{112,96},{1... | collective-permute-start | bytes 786440 | tf_op jit(solution)/shard_map/ppermute | solution.py:143
  2.2 13.5 %collective-permute-start.2 = (f32[1,4,64,128]{3,2,1,0:T(8,128)}, f32[1,4,64,128]{3,2,1,0:T(8,128)S(1)}, u32[]{:S(2)}, u32[]{:S(2)}) collective-permute-start(f32[1,4,64,128]{3,2,1,0:T(8,128)} %source.15), channel_id=1, source_target_pairs={{0,16},{16,0},{32,48},{48,32},{64,80},{80,64},{96,112},{112,96},{1... | collective-permute-start | bytes 393224 | tf_op jit(solution)/shard_map/ppermute | solution.py:143
  2.6 13.0 %collective-permute-start = (s32[1,94]{1,0:T(1,128)}, s32[1,94]{1,0:T(1,128)S(1)}, u32[]{:S(2)}, u32[]{:S(2)}) collective-permute-start(s32[1,94]{1,0:T(1,128)} %rows.15), channel_id=1, source_target_pairs={{0,16},{16,0},{32,48},{48,32},{64,80},{80,64},{96,112},{112,96},{1... | collective-permute-start | bytes 1136 | tf_op jit(solution)/shard_map/ppermute | solution.py:143
  2.7 13.0 %collective-permute-start.1 = (s32[1,94]{1,0:T(1,128)}, s32[1,94]{1,0:T(1,128)S(1)}, u32[]{:S(2)}, u32[]{:S(2)}) collective-permute-start(s32[1,94]{1,0:T(1,128)} %cols.15), channel_id=1, source_target_pairs={{0,16},{16,0},{32,48},{48,32},{64,80},{80,64},{96,112},{112,96},{1... | collective-permute-start | bytes 1136 | tf_op jit(solution)/shard_map/ppermute | solution.py:143
  3.1 2.7 %copy-start.1 = (f32[1,94,128,128]{3,2,1,0:T(8,128)S(1)}, f32[1,94,128,128]{3,2,1,0:T(8,128)}, u32[]{:S(2)}) copy-start(f32[1,94,128,128]{3,2,1,0:T(8,128)} %param.7) | copy-start | bytes 18481156
  5.9 2.9 %copy-start.2 = (f32[1,4,128,128]{3,2,1,0:T(8,128)S(1)}, f32[1,4,128,128]{3,2,1,0:T(8,128)}, u32[]{:S(2)}) copy-start(f32[1,4,128,128]{3,2,1,0:T(8,128)} %param.6) | copy-start | bytes 786436
  12.7 3.0 %copy-start = (f32[1,4,64,128]{3,2,1,0:T(8,128)S(1)}, f32[1,4,64,128]{3,2,1,0:T(8,128)}, u32[]{:S(2)}) copy-start(f32[1,4,64,128]{3,2,1,0:T(8,128)} %source.15) | copy-start | bytes 393220
  12.7 3.0 %copy-start.3 = (s32[1,94]{1,0:T(1,128)S(1)}, s32[1,94]{1,0:T(1,128)}, u32[]{:S(2)}) copy-start(s32[1,94]{1,0:T(1,128)} %rows.15) | copy-start | bytes 1132
  12.7 3.0 %copy-start.4 = (s32[1,94]{1,0:T(1,128)S(1)}, s32[1,94]{1,0:T(1,128)}, u32[]{:S(2)}) copy-start(s32[1,94]{1,0:T(1,128)} %cols.15) | copy-start | bytes 1132
  63.8 4.5 %collective-permute-start.5 = (f32[4,32,128]{2,1,0:T(8,128)S(1)}, f32[4,32,128]{2,1,0:T(8,128)S(1)}, u32[]{:S(2)}, u32[]{:S(2)}) collective-permute-start(f32[4,32,128]{2,1,0:T(8,128)S(1)} %gather_sum.4), channel_id=1, source_target_pairs={{0,32},{16,48},{32,64},{48,80},{64,96},{80,112},{96,0},{112,16},{1... | collective-permute-start | bytes 196616 | tf_op jit(solution)/shard_map/ppermute | solution.py:171
  106.1 4.6 %collective-permute-start.6 = (f32[4,32,128]{2,1,0:T(8,128)S(1)}, f32[4,32,128]{2,1,0:T(8,128)S(1)}, u32[]{:S(2)}, u32[]{:S(2)}) collective-permute-start(f32[4,32,128]{2,1,0:T(8,128)S(1)} %gather_sum.5), channel_id=1, source_target_pairs={{0,32},{16,48},{32,64},{48,80},{64,96},{80,112},{96,0},{112,16},{1... | collective-permute-start | bytes 196616 | tf_op jit(solution)/shard_map/ppermute | solution.py:171
  145.1 4.7 %collective-permute-start.7 = (f32[4,32,128]{2,1,0:T(8,128)S(1)}, f32[4,32,128]{2,1,0:T(8,128)S(1)}, u32[]{:S(2)}, u32[]{:S(2)}) collective-permute-start(f32[4,32,128]{2,1,0:T(8,128)S(1)} %gather_sum.6), channel_id=1, source_target_pairs={{0,32},{16,48},{32,64},{48,80},{64,96},{80,112},{96,0},{112,16},{1... | collective-permute-start | bytes 196616 | tf_op jit(solution)/shard_map/ppermute | solution.py:171
  169.7 15.8 %all-to-all-start.7 = ((f32[16,4,32,128]{3,2,1,0:T(8,128)}), f32[16,4,32,128]{3,2,1,0:T(8,128)S(1)}, u32[]{:S(2)}, u32[]{:S(2)}) async-start(f32[16,4,32,128]{3,2,1,0:T(8,128)} %bitcast.20), calls=%async_computation.7 | async-start | bytes 2097152 | tf_op jit(solution)/shard_map/all_to_all | solution.py:146
  185.6 13.0 %collective-permute-start.8 = (f32[2,4,32,128]{3,2,1,0:T(8,128)S(1)}, f32[2,4,32,128]{3,2,1,0:T(8,128)S(1)}, u32[]{:S(2)}, u32[]{:S(2)}) collective-permute-start(f32[2,4,32,128]{3,2,1,0:T(8,128)S(1)} %get-tuple-element.33), channel_id=1, source_target_pairs={{0,16},{16,0},{32,48},{48,32},{64,80},{80,64},{96,112},{112,96},{1... | collective-permute-start | bytes 393224 | tf_op jit(solution)/shard_map/ppermute | solution.py:143

commit v3 on v2

--- a/solution.py
+++ b/solution.py
@@ -9,6 +9,8 @@
 
 BF = jnp.bfloat16
 F32 = jnp.float32
+NONE, OLD, NEW = 0, 1, 2
+PACE = 15
 VMEM = pl.BlockSpec(memory_space=pltpu.VMEM)
 SMEM = pl.BlockSpec(memory_space=pltpu.SMEM)
 
@@ -42,35 +44,52 @@
     out_ref[at, size:] = low
 
 
-def prepare_body(first, tile_ref, *refs):
-    out_ref = refs[-1]
-
-    @pl.loop(0, tile_ref.shape[0], unroll=8)
+def prepare_tiles(tile_ref, out_ref, first, count):
+    @pl.loop(0, count, unroll=8)
     def _(i):
         prepare_tile(tile_ref[i], out_ref, first + i)
 
 
-def prepare(tiles, other_tiles):
-    count, size = tiles.shape[0], tiles.shape[1]
-    both = jax.ShapeDtypeStruct((2 * count, 2 * size, size), BF)
+def prepare_own_body(tile_ref, inverse_ref, out_ref, out_inverse_ref):
+    prepare_tiles(tile_ref, out_ref, 0, tile_ref.shape[0])
+    prepare_tiles(inverse_ref, out_inverse_ref, 0, inverse_ref.shape[0])
+
+
+def prepare_other_body(place, tile_ref, inverse_ref, held_ref, held_inverse_ref, out_ref, out_inverse_ref):
+    count, columns = tile_ref.shape[0], inverse_ref.shape[0]
+    prepare_tiles(tile_ref, out_ref, count, count)
+    prepare_tiles(inverse_ref, out_inverse_ref, columns, columns)
+
+    @pl.when(place[0] == 0)
+    def _():
+        prepare_tiles(tile_ref, out_ref, count, count * PACE // 16)
+
+
+def prepare(place, own, own_inverse, other, other_inverse):
+    count, size = own.shape[0], own.shape[1]
+    columns = own_inverse.shape[0]
+    shapes = (
+        jax.ShapeDtypeStruct((2 * count, 2 * size, size), BF),
+        jax.ShapeDtypeStruct((2 * columns, 2 * size, size), BF),
+    )
     grant = pltpu.CompilerParams(vmem_limit_bytes=20 << 20)
-    half = pl.pallas_call(
-        functools.partial(prepare_body, 0),
-        out_shape=both,
-        in_specs=[VMEM],
-        out_specs=VMEM,
+    held = pl.pallas_call(
+        prepare_own_body,
+        out_shape=shapes,
+        in_specs=[VMEM, VMEM],
+        out_specs=(VMEM, VMEM),
         compiler_params=grant,
-        name="prepare_first",
-    )(tiles)
+        name="prepare_own",
+    )(own, own_inverse)
     return pl.pallas_call(
-        functools.partial(prepare_body, count),
-        out_shape=both,
-        in_specs=[VMEM, VMEM],
-        out_specs=VMEM,
-        input_output_aliases={1: 0},
+        prepare_other_body,
+        out_shape=shapes,
+        in_specs=[SMEM] + [VMEM] * 4,
+        out_specs=(VMEM, VMEM),
+        input_output_aliases={3: 0, 4: 1},
         compiler_params=grant,
-        name="prepare_second",
-    )(other_tiles, half)
+        name="prepare_other",
+    )(place, other, other_inverse, *held)
 
 
 def gather_sum_body(arrived, total):
@@ -93,9 +112,9 @@
 
 
 def stage_body(
-    place, rows, cols, other_rows, other_cols, arrived, source, other_source, inverse, factor, sums, solved, inbound, current
+    place, rows, cols, other_rows, other_cols, arrived, before, source, other_source, inverse, factor, sums, solved, inbound, current
 ):
-    slot, live, first, shift = place[0], place[1], place[2], place[3]
+    slot, origin, first, shift = place[0], place[1], place[2], place[3]
     tiles = factor.shape[0] // 2
     columns, width = inbound.shape[0], inbound.shape[1]
     here = pl.ds(pl.multiple_of(first, width), width)
@@ -104,7 +123,8 @@
         total = arrived[0, t]
         for j in range(1, arrived.shape[0]):
             total = total + arrived[j, t]
-        total = jnp.where(live > 0, total, jnp.zeros_like(total))
+        if before is not None:
+            total = jnp.where(origin == NEW, total, jnp.where(origin == OLD, before[0, t], jnp.zeros_like(total)))
         inbound[t] = total
         right = jnp.where(slot > 0, other_source[0, t, here], source[0, t, here]) - total
         value = product(left_side(right), inverse[slot * columns + t])
@@ -117,25 +137,32 @@
         sums[row] += product(current[col], factor[base + k])
 
 
-def stage(place, tables, arrived, inputs, tile_rows):
+def stage(place, tables, arrived, before, inputs, tile_rows):
+    body = stage_body
+    if before is None:
+
+        def body(*refs):
+            stage_body(*refs[:6], None, *refs[6:])
+
+    arrivals = (arrived,) if before is None else (arrived, before)
     small = jax.ShapeDtypeStruct(arrived.shape[1:], F32)
     columns, width, size = small.shape
     return pl.pallas_call(
-        stage_body,
+        body,
         out_shape=(jax.ShapeDtypeStruct((tile_rows, width, size), F32), small, small),
-        in_specs=[SMEM] * 5 + [VMEM] * 5,
+        in_specs=[SMEM] * 5 + [VMEM] * (len(arrivals) + 4),
         out_specs=[VMEM, VMEM, VMEM],
         scratch_shapes=[pltpu.VMEM((columns, 2 * width, 2 * size), BF)],
         compiler_params=pltpu.CompilerParams(vmem_limit_bytes=6 << 20),
         name="stage",
-    )(place, *tables, arrived, *inputs)
+    )(place, *tables, *arrivals, *inputs)
 
 
 def local(sources, diag_inverse, factor_tiles, tile_rows, tile_cols):
     group = lax.axis_index("chain")
     groups = lax.axis_size("chain")
     peers = lax.axis_size("col")
-    core = lax.rem(group, 2)
+    core = group % 2
     columns = sources.shape[1]
     width = sources.shape[2] // 2
 
@@ -147,28 +174,36 @@
 
     lowest = core * width
     shift = lax.axis_index("col") * columns
-    live = jnp.where(group > 1, 1, 0)
-    place = [jnp.stack([core, live, lowest, shift]), jnp.stack([1 - core, jnp.ones_like(live), lowest, shift])]
+    plane = group // 2
+    origin = jnp.where(plane == 0, NONE, NEW)
+    last = jnp.where(plane == 2, OLD, origin)
+    place = [
+        jnp.stack([core, origin, lowest, shift]),
+        jnp.stack([core, last, lowest, shift]),
+        jnp.stack([1 - core, origin, lowest, shift]),
+    ]
     place, factor_tiles = lax.optimization_barrier((place, factor_tiles))
 
-    other_factor = swap(factor_tiles[0])
     other_inverse = swap(diag_inverse[0])
     tables = (tile_rows, tile_cols, swap(tile_rows), swap(tile_cols))
-    inputs = (
-        sources,
-        swap(sources),
-        prepare(diag_inverse[0], other_inverse),
-        prepare(factor_tiles[0], other_factor),
-    )
-
+    other_sources = swap(sources)
+    other_factor = swap(factor_tiles[0])
+    factor, inverse = prepare(place[0], factor_tiles[0], diag_inverse[0], other_factor, other_inverse)
+    inputs = (sources, other_sources, inverse, factor)
+
+    trades = [{0: 1, 1: 0, 2: 3, 3: 2}, {0: 3, 1: 2, 2: 1, 3: 0}, {0: 1, 1: 0, 2: 3, 3: 2}]
     arrived = jnp.zeros((1, columns, width, sources.shape[3]), F32)
+    before = arrived
     planes = groups // 2
     for sweep in range(planes):
-        sums, solved_even, _ = stage(place[0], tables, arrived, inputs, peers * columns)
-        sums, solved_odd, leaving_even = stage(place[1], tables, exchange(sums), inputs, peers * columns)
+        here = place[1] if sweep == planes - 1 else place[0]
+        sums, solved_even, _ = stage(here, tables, arrived, before, inputs, peers * columns)
+        sums, solved_odd, leaving_even = stage(place[2], tables, exchange(sums), None, inputs, peers * columns)
         leaving_odd = gather_sum(exchange(sums))
         if sweep < planes - 1:
-            arrived = lax.ppermute(leaving_odd, "chain", [(i, (i + 2) % groups) for i in range(groups)])[None]
+            trade = trades[sweep]
+            route = [(i, 2 * trade[i // 2] + i % 2) for i in range(groups)]
+            before, arrived = arrived, lax.ppermute(leaving_odd, "chain", route)[None]
 
     first = core == 0
     even = jnp.stack([solved_even, leaving_even])

time: 200 us -> 193 us (0.965)
  blocking collectives: 119 us -> 111 us
  starting transfers between devices: 19.6 us -> 25.6 us
  waiting for transfers between devices: 28.5 us -> 23.1 us
    all_to_all x7, blocking collectives: 119 us -> 111 us  [exchange(): lax.all_to_all(x.reshape((peers, columns) + x.shape[1:]), 'col', 0, 0)]
    ppermute x3, waiting for transfers between devices: 12.3 us -> 7.46 us  [local(): before, arrived = (arrived, lax.ppermute(leaving_odd, 'chain', route)[None])]
    ppermute x6, starting transfers between devices: 14.5 us -> 17.6 us  [swap(): return lax.ppermute(x, 'chain', [(i, i ^ 1) for i in range(groups)])]
    ppermute x3, starting transfers between devices: 1.51 us -> 4.35 us  [local(): before, arrived = (arrived, lax.ppermute(leaving_odd, 'chain', route)[None])]
    pallas_call x12 -> x10, Pallas kernels: 27.1 us -> 27.7 us  [the longest x8 20.5 us: stage(): pl.pallas_call(body, out_shape=(jax.ShapeDtypeStruct((tile_rows, width, s...]
  transfers between devices with their start and end apart: 10 -> 10, of which waited for: 6 -> 6; matrix products, arithmetic and copies ran while one was open for 0% -> 0% of each run, Pallas kernels for 3% -> 4%
where the time goes in v3:
time: 193 us
  blocking collectives  111 us (58%)
  Pallas kernels  27.9 us (14%)
  starting transfers between devices  25.6 us (13%)
  waiting for transfers between devices  23.1 us (12%)
  local copies, waits for them, and re-layouts  4.43 us (2%)
    all_to_all x7, blocking collectives, exchange(): lax.all_to_all(x.reshape((peers, columns) + x.shape[1:]), 'col', 0, 0)  111 us
    pallas_call x8, Pallas kernels, stage(): pl.pallas_call(body, out_shape=(jax.ShapeDtypeStruct((tile_rows, width, s...  20.5 us
    ppermute x6, starting transfers between devices, swap(): return lax.ppermute(x, 'chain', [(i, i ^ 1) for i in range(groups)])  17.6 us
    all_to_all x1, waiting for transfers between devices, exchange(): lax.all_to_all(x.reshape((peers, columns) + x.shape[1:]), 'col', 0, 0)  12.5 us
    ppermute x3, waiting for transfers between devices, local(): before, arrived = (arrived, lax.ppermute(leaving_odd, 'chain', route)[None])  7.46 us
    ppermute x3, starting transfers between devices, local(): before, arrived = (arrived, lax.ppermute(leaving_odd, 'chain', route)[None])  4.35 us
  transfers between devices with their start and end apart: 10, of which 6 were waited for; matrix products, arithmetic and copies ran while one was open for 0% of the time, Pallas kernels for 4%

profile of v3, /device:TPU:1, one launch (start us, length us, event | category | flops | bytes accessed | tf_op | source)
XLA Modules:
  0.0 192.9 jit_solution(14455681788320000365)
XLA Ops:
  0.7 0.1 add_add_fusion.1.place
  0.7 0.1 add_add_fusion
  0.8 1.4 collective-permute-start.3
  2.2 0.1 collective-permute-start.4
  2.3 0.4 collective-permute-start.2
  2.7 0.1 collective-permute-start
  2.9 0.4 collective-permute-start.1
  3.2 2.7 %copy-done.1 = f32[1,94,128,128]{3,2,1,0:T(8,128)S(1)} copy-done((f32[1,94,128,128]{3,2,1,0:T(8,128)S(1)}, f32[1,94,128,128]{3,2,1,0:T(8,128)}, u32[]{:S(2)}) %copy-start.1) | copy-done | bytes 6160408
  6.0 0.9 copy-done.2
  6.9 3.3 %prepare_own.1 = (bf16[188,256,128]{2,1,0:T(8,128)(2,1)S(1)}, bf16[8,256,128]{2,1,0:T(8,128)(2,1)S(1)}) custom-call(f32[94,128,128]{2,1,0:T(8,128)S(1)} %bitcast.24, f32[4,128,128]{2,1,0:T(8,128)S(1)} %bitcast.37), custom_call_target="tpu_custom_call" | custom-call | tf_op jit(solution)/shard_map/prepare_own/pallas_call | solution.py:76
  10.3 2.1 %collective-permute-done.4.inverse_ref = f32[4,128,128]{2,1,0:T(8,128)S(1)} collective-permute-done((f32[4,128,128]{2,1,0:T(8,128)}, f32[4,128,128]{2,1,0:T(8,128)S(1)}, u32[]{:S(2)}, u32[]{:S(2)}) %collective-permute-start.4) | collective-permute-done | bytes 262176 | tf_op jit(solution)/shard_map/ppermute | solution.py:170
  12.4 0.0 collective-permute-done.3.tile_ref
  12.4 3.9 %prepare_other.1 = (bf16[188,256,128]{2,1,0:T(8,128)(2,1)S(1)}, bf16[8,256,128]{2,1,0:T(8,128)(2,1)S(1)}) custom-call(s32[4]{0:T(128)S(1)} %get-tuple-element.23.place, f32[94,128,128]{2,1,0:T(8,128)S(1)} %collective-permute-done.3.tile_ref, f32[4,128,128]{2,1,0:T(8,128)S(1)} %collective-permute-done.4.inverse_ref, ...), custom_call_target="tpu_custom_call", output_to_operand_aliasing={{0}: (3, {}), {1}: (4, {})} | custom-call | tf_op jit(solution)/shard_map/prepare_other/pallas_call | solution.py:84
  16.3 0.0 collective-permute-done.other_rows.refs_3_
  16.3 0.0 collective-permute-done.1.other_cols.refs_4_
  16.3 0.0 collective-permute-done.2.other_source.refs_7_
  16.3 0.0 copy-done.3
  16.3 0.0 copy-done.4
  16.3 2.5 %stage.8 = (f32[64,32,128]{2,1,0:T(8,128)S(1)}, f32[4,32,128]{2,1,0:T(8,128)}, f32[4,32,128]{2,1,0:T(8,128)}) custom-call(s32[4]{0:T(128)S(1)} %get-tuple-element.23.place, s32[1,94]{1,0:T(1,128)S(1)} %copy-done.3, s32[1,94]{1,0:T(1,128)S(1)} %copy-done.4, s32[1,94]{1,0:T(1,128)S(1)} %collective-permute-done.other_rows.refs_3_, ...), custom_call_target="tpu_custom_call" | custom-call | tf_op jit(solution)/shard_map/stage/pallas_call | solution.py:150
  18.9 21.6 %all_to_all.40.refs_5_ = f32[16,4,32,128]{3,2,1,0:T(8,128)S(1)} all-to-all(f32[16,4,32,128]{3,2,1,0:T(8,128)S(1)} %bitcast.31), channel_id=1, replica_groups=mesh['chain'=8,'col'=16] {'col'}, dimensions={0} | all-to-all | bytes 2097152 | tf_op jit(solution)/shard_map/all_to_all | solution.py:173
  40.5 2.5 %stage.9 = (f32[64,32,128]{2,1,0:T(8,128)S(1)}, f32[4,32,128]{2,1,0:T(8,128)}, f32[4,32,128]{2,1,0:T(8,128)}) custom-call(s32[4]{0:T(128)S(1)} %get-tuple-element.22.refs_0_, s32[1,94]{1,0:T(1,128)S(1)} %copy-done.3, s32[1,94]{1,0:T(1,128)S(1)} %copy-done.4, s32[1,94]{1,0:T(1,128)S(1)} %collective-permute-done.other_rows.refs_3_, ...), custom_call_target="tpu_custom_call" | custom-call | tf_op jit(solution)/shard_map/stage/pallas_call | solution.py:150
  43.0 16.3 %all_to_all.41.arrived = f32[16,4,32,128]{3,2,1,0:T(8,128)S(1)} all-to-all(f32[16,4,32,128]{3,2,1,0:T(8,128)S(1)} %bitcast.27), channel_id=1, replica_groups=mesh['chain'=8,'col'=16] {'col'}, dimensions={0} | all-to-all | bytes 2097152 | tf_op jit(solution)/shard_map/all_to_all | solution.py:173
  59.3 0.1 gather_sum.4
  59.4 1.4 collective-permute-start.5
  60.8 2.1 %collective-permute-done.5 = f32[4,32,128]{2,1,0:T(8,128)S(1)} collective-permute-done((f32[4,32,128]{2,1,0:T(8,128)S(1)}, f32[4,32,128]{2,1,0:T(8,128)S(1)}, u32[]{:S(2)}, u32[]{:S(2)}) %collective-permute-start.5) | collective-permute-done | bytes 65568 | tf_op jit(solution)/shard_map/ppermute | solution.py:206
  62.9 2.5 %stage.10 = (f32[64,32,128]{2,1,0:T(8,128)S(1)}, f32[4,32,128]{2,1,0:T(8,128)}, f32[4,32,128]{2,1,0:T(8,128)}) custom-call(s32[4]{0:T(128)S(1)} %get-tuple-element.23.place, s32[1,94]{1,0:T(1,128)S(1)} %copy-done.3, s32[1,94]{1,0:T(1,128)S(1)} %copy-done.4, s32[1,94]{1,0:T(1,128)S(1)} %collective-permute-done.other_rows.refs_3_, ...), custom_call_target="tpu_custom_call" | custom-call | tf_op jit(solution)/shard_map/stage/pallas_call | solution.py:150
  65.4 14.9 %all_to_all.42.refs_5_ = f32[16,4,32,128]{3,2,1,0:T(8,128)S(1)} all-to-all(f32[16,4,32,128]{3,2,1,0:T(8,128)S(1)} %bitcast.28), channel_id=1, replica_groups=mesh['chain'=8,'col'=16] {'col'}, dimensions={0} | all-to-all | bytes 2097152 | tf_op jit(solution)/shard_map/all_to_all | solution.py:173
  80.3 2.5 %stage.11 = (f32[64,32,128]{2,1,0:T(8,128)S(1)}, f32[4,32,128]{2,1,0:T(8,128)}, f32[4,32,128]{2,1,0:T(8,128)}) custom-call(s32[4]{0:T(128)S(1)} %get-tuple-element.22.refs_0_, s32[1,94]{1,0:T(1,128)S(1)} %copy-done.3, s32[1,94]{1,0:T(1,128)S(1)} %copy-done.4, s32[1,94]{1,0:T(1,128)S(1)} %collective-permute-done.other_rows.refs_3_, ...), custom_call_target="tpu_custom_call" | custom-call | tf_op jit(solution)/shard_map/stage/pallas_call | solution.py:150
  82.8 14.5 %all_to_all.43.arrived = f32[16,4,32,128]{3,2,1,0:T(8,128)S(1)} all-to-all(f32[16,4,32,128]{3,2,1,0:T(8,128)S(1)} %bitcast.29), channel_id=1, replica_groups=mesh['chain'=8,'col'=16] {'col'}, dimensions={0} | all-to-all | bytes 2097152 | tf_op jit(solution)/shard_map/all_to_all | solution.py:173
  97.2 0.1 gather_sum.5
  97.3 2.9 %collective-permute-start.6 = (f32[4,32,128]{2,1,0:T(8,128)S(1)}, f32[4,32,128]{2,1,0:T(8,128)S(1)}, u32[]{:S(2)}, u32[]{:S(2)}) collective-permute-start(f32[4,32,128]{2,1,0:T(8,128)S(1)} %gather_sum.5), channel_id=1, source_target_pairs={{0,96},{16,112},{32,64},{48,80},{64,32},{80,48},{96,0},{112,16},{1... | collective-permute-start | bytes 196616 | tf_op jit(solution)/shard_map/ppermute | solution.py:206
  100.2 2.0 %collective-permute-done.6 = f32[4,32,128]{2,1,0:T(8,128)S(1)} collective-permute-done((f32[4,32,128]{2,1,0:T(8,128)S(1)}, f32[4,32,128]{2,1,0:T(8,128)S(1)}, u32[]{:S(2)}, u32[]{:S(2)}) %collective-permute-start.6) | collective-permute-done | bytes 65568 | tf_op jit(solution)/shard_map/ppermute | solution.py:206
  102.1 2.5 %stage.12 = (f32[64,32,128]{2,1,0:T(8,128)S(1)}, f32[4,32,128]{2,1,0:T(8,128)}, f32[4,32,128]{2,1,0:T(8,128)}) custom-call(s32[4]{0:T(128)S(1)} %get-tuple-element.23.place, s32[1,94]{1,0:T(1,128)S(1)} %copy-done.3, s32[1,94]{1,0:T(1,128)S(1)} %copy-done.4, s32[1,94]{1,0:T(1,128)S(1)} %collective-permute-done.other_rows.refs_3_, ...), custom_call_target="tpu_custom_call" | custom-call | tf_op jit(solution)/shard_map/stage/pallas_call | solution.py:150
  104.6 14.5 %all_to_all.44.refs_5_ = f32[16,4,32,128]{3,2,1,0:T(8,128)S(1)} all-to-all(f32[16,4,32,128]{3,2,1,0:T(8,128)S(1)} %bitcast.26), channel_id=1, replica_groups=mesh['chain'=8,'col'=16] {'col'}, dimensions={0} | all-to-all | bytes 2097152 | tf_op jit(solution)/shard_map/all_to_all | solution.py:173
  119.1 2.5 %stage.13 = (f32[64,32,128]{2,1,0:T(8,128)S(1)}, f32[4,32,128]{2,1,0:T(8,128)}, f32[4,32,128]{2,1,0:T(8,128)}) custom-call(s32[4]{0:T(128)S(1)} %get-tuple-element.22.refs_0_, s32[1,94]{1,0:T(1,128)S(1)} %copy-done.3, s32[1,94]{1,0:T(1,128)S(1)} %copy-done.4, s32[1,94]{1,0:T(1,128)S(1)} %collective-permute-done.other_rows.refs_3_, ...), custom_call_target="tpu_custom_call" | custom-call | tf_op jit(solution)/shard_map/stage/pallas_call | solution.py:150
  121.6 14.6 %all_to_all.45.arrived = f32[16,4,32,128]{3,2,1,0:T(8,128)S(1)} all-to-all(f32[16,4,32,128]{3,2,1,0:T(8,128)S(1)} %bitcast.30), channel_id=1, replica_groups=mesh['chain'=8,'col'=16] {'col'}, dimensions={0} | all-to-all | bytes 2097152 | tf_op jit(solution)/shard_map/all_to_all | solution.py:173
  136.2 0.1 gather_sum.6
  136.3 0.1 collective-permute-start.7
  136.4 3.4 %collective-permute-done.7 = f32[4,32,128]{2,1,0:T(8,128)S(1)} collective-permute-done((f32[4,32,128]{2,1,0:T(8,128)S(1)}, f32[4,32,128]{2,1,0:T(8,128)S(1)}, u32[]{:S(2)}, u32[]{:S(2)}) %collective-permute-start.7) | collective-permute-done | bytes 65568 | tf_op jit(solution)/shard_map/ppermute | solution.py:206
  139.8 2.5 %stage.14 = (f32[64,32,128]{2,1,0:T(8,128)S(1)}, f32[4,32,128]{2,1,0:T(8,128)S(1)}, f32[4,32,128]{2,1,0:T(8,128)}) custom-call(s32[4]{0:T(128)S(1)} %add_add_fusion.1.place, s32[1,94]{1,0:T(1,128)S(1)} %copy-done.3, s32[1,94]{1,0:T(1,128)S(1)} %copy-done.4, s32[1,94]{1,0:T(1,128)S(1)} %collective-permute-done.other_rows.refs_3_, ...), custom_call_target="tpu_custom_call" | custom-call | tf_op jit(solution)/shard_map/stage/pallas_call | solution.py:150
  142.3 14.5 %all_to_all.46.refs_5_ = f32[16,4,32,128]{3,2,1,0:T(8,128)S(1)} all-to-all(f32[16,4,32,128]{3,2,1,0:T(8,128)S(1)} %bitcast.25), channel_id=1, replica_groups=mesh['chain'=8,'col'=16] {'col'}, dimensions={0} | all-to-all | bytes 2097152 | tf_op jit(solution)/shard_map/all_to_all | solution.py:173
  156.7 3.0 %stage.15 = (f32[64,32,128]{2,1,0:T(8,128)}, f32[4,32,128]{2,1,0:T(8,128)S(1)}, f32[4,32,128]{2,1,0:T(8,128)S(1)}) custom-call(s32[4]{0:T(128)S(1)} %get-tuple-element.22.refs_0_, s32[1,94]{1,0:T(1,128)S(1)} %copy-done.3, s32[1,94]{1,0:T(1,128)S(1)} %copy-done.4, s32[1,94]{1,0:T(1,128)S(1)} %collective-permute-done.other_rows.refs_3_, ...), custom_call_target="tpu_custom_call" | custom-call | tf_op jit(solution)/shard_map/stage/pallas_call | solution.py:150
  159.7 3.7 %all-to-all-start.7 = ((f32[16,4,32,128]{3,2,1,0:T(8,128)}), f32[16,4,32,128]{3,2,1,0:T(8,128)S(1)}, u32[]{:S(2)}, u32[]{:S(2)}) async-start(f32[16,4,32,128]{3,2,1,0:T(8,128)} %bitcast.21), calls=%async_computation.7 | async-start | bytes 2097152 | tf_op jit(solution)/shard_map/all_to_all | solution.py:173
  163.4 12.5 %all-to-all-done.7.arrived = f32[16,4,32,128]{3,2,1,0:T(8,128)S(1)} async-done(((f32[16,4,32,128]{3,2,1,0:T(8,128)}), f32[16,4,32,128]{3,2,1,0:T(8,128)S(1)}, u32[]{:S(2)}, u32[]{:S(2)}) %all-to-all-start.7) | async-done | bytes 1048608 | tf_op jit(solution)/shard_map/all_to_all | solution.py:173
  175.9 0.1 gather_sum.7
  176.0 15.1 %collective-permute-start.8 = (f32[2,4,32,128]{3,2,1,0:T(8,128)S(1)}, f32[2,4,32,128]{3,2,1,0:T(8,128)S(1)}, u32[]{:S(2)}, u32[]{:S(2)}) collective-permute-start(f32[2,4,32,128]{3,2,1,0:T(8,128)S(1)} %get-tuple-element.43), channel_id=1, source_target_pairs={{0,16},{16,0},{32,48},{48,32},{64,80},{80,64},{96,112},{112,96},{1... | collective-permute-start | bytes 393224 | tf_op jit(solution)/shard_map/ppermute | solution.py:170
  191.1 1.0 collective-permute-done.8
  192.1 0.7 fusion.2
  (9 shorter events, 0.1 us)
Async XLA Ops:
  0.8 11.6 %collective-permute-start.3 = (f32[94,128,128]{2,1,0:T(8,128)}, f32[94,128,128]{2,1,0:T(8,128)S(1)}, u32[]{:S(2)}, u32[]{:S(2)}) collective-permute-start(f32[94,128,128]{2,1,0:T(8,128)} %bitcast.23), channel_id=1, source_target_pairs={{0,16},{16,0},{32,48},{48,32},{64,80},{80,64},{96,112},{112,96},{1... | collective-permute-start | bytes 18481160 | tf_op jit(solution)/shard_map/ppermute | solution.py:170
  2.2 14.1 %copy-start.3 = (s32[1,94]{1,0:T(1,128)S(1)}, s32[1,94]{1,0:T(1,128)}, u32[]{:S(2)}) copy-start(s32[1,94]{1,0:T(1,128)} %refs_1_.7) | copy-start | bytes 1132
  2.2 14.1 %copy-start.4 = (s32[1,94]{1,0:T(1,128)S(1)}, s32[1,94]{1,0:T(1,128)}, u32[]{:S(2)}) copy-start(s32[1,94]{1,0:T(1,128)} %refs_2_.7) | copy-start | bytes 1132
  2.2 14.1 %copy-start = (f32[1,4,64,128]{3,2,1,0:T(8,128)S(1)}, f32[1,4,64,128]{3,2,1,0:T(8,128)}, u32[]{:S(2)}) copy-start(f32[1,4,64,128]{3,2,1,0:T(8,128)} %refs_6_.7) | copy-start | bytes 393220
  2.2 10.2 %collective-permute-start.4 = (f32[4,128,128]{2,1,0:T(8,128)}, f32[4,128,128]{2,1,0:T(8,128)S(1)}, u32[]{:S(2)}, u32[]{:S(2)}) collective-permute-start(f32[4,128,128]{2,1,0:T(8,128)} %bitcast.36), channel_id=1, source_target_pairs={{0,16},{16,0},{32,48},{48,32},{64,80},{80,64},{96,112},{112,96},{1... | collective-permute-start | bytes 786440 | tf_op jit(solution)/shard_map/ppermute | solution.py:170
  2.3 13.9 %collective-permute-start.2 = (f32[1,4,64,128]{3,2,1,0:T(8,128)}, f32[1,4,64,128]{3,2,1,0:T(8,128)S(1)}, u32[]{:S(2)}, u32[]{:S(2)}) collective-permute-start(f32[1,4,64,128]{3,2,1,0:T(8,128)} %refs_6_.7), channel_id=1, source_target_pairs={{0,16},{16,0},{32,48},{48,32},{64,80},{80,64},{96,112},{112,96},{1... | collective-permute-start | bytes 393224 | tf_op jit(solution)/shard_map/ppermute | solution.py:170
  2.7 13.5 %collective-permute-start = (s32[1,94]{1,0:T(1,128)}, s32[1,94]{1,0:T(1,128)S(1)}, u32[]{:S(2)}, u32[]{:S(2)}) collective-permute-start(s32[1,94]{1,0:T(1,128)} %refs_1_.7), channel_id=1, source_target_pairs={{0,16},{16,0},{32,48},{48,32},{64,80},{80,64},{96,112},{112,96},{1... | collective-permute-start | bytes 1136 | tf_op jit(solution)/shard_map/ppermute | solution.py:170
  2.9 13.4 %collective-permute-start.1 = (s32[1,94]{1,0:T(1,128)}, s32[1,94]{1,0:T(1,128)S(1)}, u32[]{:S(2)}, u32[]{:S(2)}) collective-permute-start(s32[1,94]{1,0:T(1,128)} %refs_2_.7), channel_id=1, source_target_pairs={{0,16},{16,0},{32,48},{48,32},{64,80},{80,64},{96,112},{112,96},{1... | collective-permute-start | bytes 1136 | tf_op jit(solution)/shard_map/ppermute | solution.py:170
  3.2 2.7 %copy-start.1 = (f32[1,94,128,128]{3,2,1,0:T(8,128)S(1)}, f32[1,94,128,128]{3,2,1,0:T(8,128)}, u32[]{:S(2)}) copy-start(f32[1,94,128,128]{3,2,1,0:T(8,128)} %param.7) | copy-start | bytes 18481156
  6.0 0.9 copy-start.2
  59.4 3.5 %collective-permute-start.5 = (f32[4,32,128]{2,1,0:T(8,128)S(1)}, f32[4,32,128]{2,1,0:T(8,128)S(1)}, u32[]{:S(2)}, u32[]{:S(2)}) collective-permute-start(f32[4,32,128]{2,1,0:T(8,128)S(1)} %gather_sum.4), channel_id=1, source_target_pairs={{0,32},{16,48},{32,0},{48,16},{64,96},{80,112},{96,64},{112,80},{1... | collective-permute-start | bytes 196616 | tf_op jit(solution)/shard_map/ppermute | solution.py:206
  97.3 4.8 %collective-permute-start.6 = (f32[4,32,128]{2,1,0:T(8,128)S(1)}, f32[4,32,128]{2,1,0:T(8,128)S(1)}, u32[]{:S(2)}, u32[]{:S(2)}) collective-permute-start(f32[4,32,128]{2,1,0:T(8,128)S(1)} %gather_sum.5), channel_id=1, source_target_pairs={{0,96},{16,112},{32,64},{48,80},{64,32},{80,48},{96,0},{112,16},{1... | collective-permute-start | bytes 196616 | tf_op jit(solution)/shard_map/ppermute | solution.py:206
  136.3 3.5 %collective-permute-start.7 = (f32[4,32,128]{2,1,0:T(8,128)S(1)}, f32[4,32,128]{2,1,0:T(8,128)S(1)}, u32[]{:S(2)}, u32[]{:S(2)}) collective-permute-start(f32[4,32,128]{2,1,0:T(8,128)S(1)} %gather_sum.6), channel_id=1, source_target_pairs={{0,32},{16,48},{32,0},{48,16},{64,96},{80,112},{96,64},{112,80},{1... | collective-permute-start | bytes 196616 | tf_op jit(solution)/shard_map/ppermute | solution.py:206
  159.7 16.2 %all-to-all-start.7 = ((f32[16,4,32,128]{3,2,1,0:T(8,128)}), f32[16,4,32,128]{3,2,1,0:T(8,128)S(1)}, u32[]{:S(2)}, u32[]{:S(2)}) async-start(f32[16,4,32,128]{3,2,1,0:T(8,128)} %bitcast.21), calls=%async_computation.7 | async-start | bytes 2097152 | tf_op jit(solution)/shard_map/all_to_all | solution.py:173
  176.0 16.1 %collective-permute-start.8 = (f32[2,4,32,128]{3,2,1,0:T(8,128)S(1)}, f32[2,4,32,128]{3,2,1,0:T(8,128)S(1)}, u32[]{:S(2)}, u32[]{:S(2)}) collective-permute-start(f32[2,4,32,128]{3,2,1,0:T(8,128)S(1)} %get-tuple-element.43), channel_id=1, source_target_pairs={{0,16},{16,0},{32,48},{48,32},{64,80},{80,64},{96,112},{112,96},{1... | collective-permute-start | bytes 393224 | tf_op jit(solution)/shard_map/ppermute | solution.py:170

commit v4 on v3

--- a/solution.py
+++ b/solution.py
@@ -10,7 +10,7 @@
 BF = jnp.bfloat16
 F32 = jnp.float32
 NONE, OLD, NEW = 0, 1, 2
-PACE = 15
+LEAD, HOLD = 48, 50
 VMEM = pl.BlockSpec(memory_space=pltpu.VMEM)
 SMEM = pl.BlockSpec(memory_space=pltpu.SMEM)
 
@@ -45,8 +45,7 @@
 
 
 def prepare_tiles(tile_ref, out_ref, first, count):
-    @pl.loop(0, count, unroll=8)
-    def _(i):
+    for i in range(count):
         prepare_tile(tile_ref[i], out_ref, first + i)
 
 
@@ -55,17 +54,13 @@
     prepare_tiles(inverse_ref, out_inverse_ref, 0, inverse_ref.shape[0])
 
 
-def prepare_other_body(place, tile_ref, inverse_ref, held_ref, held_inverse_ref, out_ref, out_inverse_ref):
+def prepare_other_body(tile_ref, inverse_ref, held_ref, held_inverse_ref, out_ref, out_inverse_ref):
     count, columns = tile_ref.shape[0], inverse_ref.shape[0]
     prepare_tiles(tile_ref, out_ref, count, count)
     prepare_tiles(inverse_ref, out_inverse_ref, columns, columns)
 
-    @pl.when(place[0] == 0)
-    def _():
-        prepare_tiles(tile_ref, out_ref, count, count * PACE // 16)
-
-
-def prepare(place, own, own_inverse, other, other_inverse):
+
+def prepare(own, own_inverse, other, other_inverse):
     count, size = own.shape[0], own.shape[1]
     columns = own_inverse.shape[0]
     shapes = (
@@ -84,12 +79,12 @@
     return pl.pallas_call(
         prepare_other_body,
         out_shape=shapes,
-        in_specs=[SMEM] + [VMEM] * 4,
+        in_specs=[VMEM] * 4,
         out_specs=(VMEM, VMEM),
-        input_output_aliases={3: 0, 4: 1},
+        input_output_aliases={2: 0, 3: 1},
         compiler_params=grant,
         name="prepare_other",
-    )(place, other, other_inverse, *held)
+    )(other, other_inverse, *held)
 
 
 def gather_sum_body(arrived, total):
@@ -118,7 +113,11 @@
     tiles = factor.shape[0] // 2
     columns, width = inbound.shape[0], inbound.shape[1]
     here = pl.ds(pl.multiple_of(first, width), width)
-    sums[...] = jnp.zeros_like(sums)
+
+    @pl.loop(0, place[4])
+    def _(_):
+        sums[...] = jnp.zeros_like(sums)
+
     for t in range(columns):
         total = arrived[0, t]
         for j in range(1, arrived.shape[0]):
@@ -177,10 +176,13 @@
     plane = group // 2
     origin = jnp.where(plane == 0, NONE, NEW)
     last = jnp.where(plane == 2, OLD, origin)
+    once = jnp.ones_like(core)
     place = [
-        jnp.stack([core, origin, lowest, shift]),
-        jnp.stack([core, last, lowest, shift]),
-        jnp.stack([1 - core, origin, lowest, shift]),
+        jnp.stack([core, origin, lowest, shift, jnp.where(core == 0, LEAD, 1)]),
+        jnp.stack([core, origin, lowest, shift, once]),
+        jnp.stack([core, origin, lowest, shift, jnp.where(core == 0, 1, HOLD)]),
+        jnp.stack([core, last, lowest, shift, once]),
+        jnp.stack([1 - core, origin, lowest, shift, once]),
     ]
     place, factor_tiles = lax.optimization_barrier((place, factor_tiles))
 
@@ -188,7 +190,7 @@
     tables = (tile_rows, tile_cols, swap(tile_rows), swap(tile_cols))
     other_sources = swap(sources)
     other_factor = swap(factor_tiles[0])
-    factor, inverse = prepare(place[0], factor_tiles[0], diag_inverse[0], other_factor, other_inverse)
+    factor, inverse = prepare(factor_tiles[0], diag_inverse[0], other_factor, other_inverse)
     inputs = (sources, other_sources, inverse, factor)
 
     trades = [{0: 1, 1: 0, 2: 3, 3: 2}, {0: 3, 1: 2, 2: 1, 3: 0}, {0: 1, 1: 0, 2: 3, 3: 2}]
@@ -196,9 +198,8 @@
     before = arrived
     planes = groups // 2
     for sweep in range(planes):
-        here = place[1] if sweep == planes - 1 else place[0]
-        sums, solved_even, _ = stage(here, tables, arrived, before, inputs, peers * columns)
-        sums, solved_odd, leaving_even = stage(place[2], tables, exchange(sums), None, inputs, peers * columns)
+        sums, solved_even, _ = stage(place[sweep], tables, arrived, before, inputs, peers * columns)
+        sums, solved_odd, leaving_even = stage(place[-1], tables, exchange(sums), None, inputs, peers * columns)
         leaving_odd = gather_sum(exchange(sums))
         if sweep < planes - 1:
             trade = trades[sweep]

time: 193 us -> 189 us (0.979)
  blocking collectives: 111 us -> 124 us
  waiting for transfers between devices: 23.1 us -> 12.1 us
  starting transfers between devices: 25.6 us -> 19.5 us
    all_to_all x7 -> x8, blocking collectives: 111 us -> 124 us  [exchange(): lax.all_to_all(x.reshape((peers, columns) + x.shape[1:]), 'col', 0, 0)]
    all_to_all x1 -> x0, waiting for transfers between devices: 12.5 us -> none  [exchange(): lax.all_to_all(x.reshape((peers, columns) + x.shape[1:]), 'col', 0, 0)]
    all_to_all x1 -> x0, starting transfers between devices: 3.65 us -> none  [exchange(): lax.all_to_all(x.reshape((peers, columns) + x.shape[1:]), 'col', 0, 0)]
    pallas_call x8, Pallas kernels: 20.5 us -> 23.8 us  [stage(): pl.pallas_call(body, out_shape=(jax.ShapeDtypeStruct((tile_rows, width, s...]
    ppermute x6, starting transfers between devices: 17.6 us -> 15.1 us  [swap(): return lax.ppermute(x, 'chain', [(i, i ^ 1) for i in range(groups)])]
    pallas_call x1, Pallas kernels: 3.85 us -> 1.72 us  [prepare(): pl.pallas_call(prepare_other_body, out_shape=shapes, in_specs=[VMEM] * 4,...]
  transfers between devices with their start and end apart: 10 -> 9, of which waited for: 6 -> 5; matrix products, arithmetic and copies ran while one was open for 0% -> 0% of each run, Pallas kernels for 4% -> 2%
where the time goes in v4:
time: 189 us
  blocking collectives  124 us (66%)
  Pallas kernels  27.4 us (14%)
  starting transfers between devices  19.5 us (10%)
  waiting for transfers between devices  12.1 us (6%)
  local copies, waits for them, and re-layouts  4.85 us (3%)
    all_to_all x8, blocking collectives, exchange(): lax.all_to_all(x.reshape((peers, columns) + x.shape[1:]), 'col', 0, 0)  124 us
    pallas_call x8, Pallas kernels, stage(): pl.pallas_call(body, out_shape=(jax.ShapeDtypeStruct((tile_rows, width, s...  23.8 us
    ppermute x6, starting transfers between devices, swap(): return lax.ppermute(x, 'chain', [(i, i ^ 1) for i in range(groups)])  15.1 us
    ppermute x3, waiting for transfers between devices, local(): before, arrived = (arrived, lax.ppermute(leaving_odd, 'chain', route)[None])  7.37 us
    ppermute x6, waiting for transfers between devices, swap(): return lax.ppermute(x, 'chain', [(i, i ^ 1) for i in range(groups)])  4.73 us
    ppermute x3, starting transfers between devices, local(): before, arrived = (arrived, lax.ppermute(leaving_odd, 'chain', route)[None])  4.4 us
  transfers between devices with their start and end apart: 9, of which 5 were waited for; matrix products, arithmetic and copies ran while one was open for 0% of the time, Pallas kernels for 2%

profile of v4, /device:TPU:1, one launch (start us, length us, event | category | flops | bytes accessed | tf_op | source)
XLA Modules:
  0.0 188.6 jit_solution(1209879508377643944)
XLA Ops:
  0.7 0.1 stack.83.refs_0_
  0.8 0.1 stack.77.place
  0.8 0.1 stack.81.place
  0.9 0.1 stack.79.place
  1.0 0.1 stack.76.place
  1.1 1.4 collective-permute-start.3
  2.5 0.1 collective-permute-start.4
  2.6 0.4 collective-permute-start.2
  3.0 0.1 collective-permute-start
  3.1 0.4 collective-permute-start.1
  3.5 2.7 %copy-done.1 = f32[1,94,128,128]{3,2,1,0:T(8,128)S(1)} copy-done((f32[1,94,128,128]{3,2,1,0:T(8,128)S(1)}, f32[1,94,128,128]{3,2,1,0:T(8,128)}, u32[]{:S(2)}) %copy-start.1) | copy-done | bytes 6160408
  6.3 0.9 copy-done.2
  7.2 1.7 prepare_own.1
  8.9 3.7 %collective-permute-done.4.inverse_ref = f32[4,128,128]{2,1,0:T(8,128)S(1)} collective-permute-done((f32[4,128,128]{2,1,0:T(8,128)}, f32[4,128,128]{2,1,0:T(8,128)S(1)}, u32[]{:S(2)}, u32[]{:S(2)}) %collective-permute-start.4) | collective-permute-done | bytes 262176 | tf_op jit(solution)/shard_map/ppermute | solution.py:169
  12.7 0.0 collective-permute-done.3.tile_ref
  12.7 1.7 prepare_other.1
  14.4 0.0 collective-permute-done.other_rows.refs_3_
  14.4 0.0 collective-permute-done.1.other_cols.refs_4_
  14.4 0.0 collective-permute-done.2.other_source.refs_7_
  14.5 2.6 %stage.8 = (f32[64,32,128]{2,1,0:T(8,128)S(1)}, f32[4,32,128]{2,1,0:T(8,128)}, f32[4,32,128]{2,1,0:T(8,128)}) custom-call(s32[5]{0:T(128)S(1)} %stack.76.place, s32[1,94]{1,0:T(1,128)S(1)} %copy-done.3, s32[1,94]{1,0:T(1,128)S(1)} %copy-done.4, s32[1,94]{1,0:T(1,128)S(1)} %collective-permute-done.other_rows.refs_3_, ...), custom_call_target="tpu_custom_call" | custom-call | tf_op jit(solution)/shard_map/stage/pallas_call | solution.py:149
  17.1 20.8 %all_to_all.40.refs_5_ = f32[16,4,32,128]{3,2,1,0:T(8,128)S(1)} all-to-all(f32[16,4,32,128]{3,2,1,0:T(8,128)S(1)} %bitcast.31), channel_id=1, replica_groups=mesh['chain'=8,'col'=16] {'col'}, dimensions={0} | all-to-all | bytes 2097152 | tf_op jit(solution)/shard_map/all_to_all | solution.py:172
  37.9 2.6 %stage.9 = (f32[64,32,128]{2,1,0:T(8,128)S(1)}, f32[4,32,128]{2,1,0:T(8,128)}, f32[4,32,128]{2,1,0:T(8,128)}) custom-call(s32[5]{0:T(128)S(1)} %stack.83.refs_0_, s32[1,94]{1,0:T(1,128)S(1)} %copy-done.3, s32[1,94]{1,0:T(1,128)S(1)} %copy-done.4, s32[1,94]{1,0:T(1,128)S(1)} %collective-permute-done.other_rows.refs_3_, ...), custom_call_target="tpu_custom_call" | custom-call | tf_op jit(solution)/shard_map/stage/pallas_call | solution.py:149
  40.5 16.1 %all_to_all.41.arrived = f32[16,4,32,128]{3,2,1,0:T(8,128)S(1)} all-to-all(f32[16,4,32,128]{3,2,1,0:T(8,128)S(1)} %bitcast.32), channel_id=1, replica_groups=mesh['chain'=8,'col'=16] {'col'}, dimensions={0} | all-to-all | bytes 2097152 | tf_op jit(solution)/shard_map/all_to_all | solution.py:172
  56.6 0.1 gather_sum.4
  56.7 1.4 collective-permute-start.5
  58.1 2.1 %collective-permute-done.5 = f32[4,32,128]{2,1,0:T(8,128)S(1)} collective-permute-done((f32[4,32,128]{2,1,0:T(8,128)S(1)}, f32[4,32,128]{2,1,0:T(8,128)S(1)}, u32[]{:S(2)}, u32[]{:S(2)}) %collective-permute-start.5) | collective-permute-done | bytes 65568 | tf_op jit(solution)/shard_map/ppermute | solution.py:207
  60.2 2.6 %stage.10 = (f32[64,32,128]{2,1,0:T(8,128)S(1)}, f32[4,32,128]{2,1,0:T(8,128)}, f32[4,32,128]{2,1,0:T(8,128)}) custom-call(s32[5]{0:T(128)S(1)} %stack.77.place, s32[1,94]{1,0:T(1,128)S(1)} %copy-done.3, s32[1,94]{1,0:T(1,128)S(1)} %copy-done.4, s32[1,94]{1,0:T(1,128)S(1)} %collective-permute-done.other_rows.refs_3_, ...), custom_call_target="tpu_custom_call" | custom-call | tf_op jit(solution)/shard_map/stage/pallas_call | solution.py:149
  62.8 14.5 %all_to_all.42.refs_5_ = f32[16,4,32,128]{3,2,1,0:T(8,128)S(1)} all-to-all(f32[16,4,32,128]{3,2,1,0:T(8,128)S(1)} %bitcast.29), channel_id=1, replica_groups=mesh['chain'=8,'col'=16] {'col'}, dimensions={0} | all-to-all | bytes 2097152 | tf_op jit(solution)/shard_map/all_to_all | solution.py:172
  77.3 2.6 %stage.11 = (f32[64,32,128]{2,1,0:T(8,128)S(1)}, f32[4,32,128]{2,1,0:T(8,128)}, f32[4,32,128]{2,1,0:T(8,128)}) custom-call(s32[5]{0:T(128)S(1)} %stack.83.refs_0_, s32[1,94]{1,0:T(1,128)S(1)} %copy-done.3, s32[1,94]{1,0:T(1,128)S(1)} %copy-done.4, s32[1,94]{1,0:T(1,128)S(1)} %collective-permute-done.other_rows.refs_3_, ...), custom_call_target="tpu_custom_call" | custom-call | tf_op jit(solution)/shard_map/stage/pallas_call | solution.py:149
  79.9 14.6 %all_to_all.43.arrived = f32[16,4,32,128]{3,2,1,0:T(8,128)S(1)} all-to-all(f32[16,4,32,128]{3,2,1,0:T(8,128)S(1)} %bitcast.33), channel_id=1, replica_groups=mesh['chain'=8,'col'=16] {'col'}, dimensions={0} | all-to-all | bytes 2097152 | tf_op jit(solution)/shard_map/all_to_all | solution.py:172
  94.5 0.1 gather_sum.5
  94.6 2.8 %collective-permute-start.6 = (f32[4,32,128]{2,1,0:T(8,128)S(1)}, f32[4,32,128]{2,1,0:T(8,128)S(1)}, u32[]{:S(2)}, u32[]{:S(2)}) collective-permute-start(f32[4,32,128]{2,1,0:T(8,128)S(1)} %gather_sum.5), channel_id=1, source_target_pairs={{0,96},{16,112},{32,64},{48,80},{64,32},{80,48},{96,0},{112,16},{1... | collective-permute-start | bytes 196616 | tf_op jit(solution)/shard_map/ppermute | solution.py:207
  97.4 2.0 %collective-permute-done.6 = f32[4,32,128]{2,1,0:T(8,128)S(1)} collective-permute-done((f32[4,32,128]{2,1,0:T(8,128)S(1)}, f32[4,32,128]{2,1,0:T(8,128)S(1)}, u32[]{:S(2)}, u32[]{:S(2)}) %collective-permute-start.6) | collective-permute-done | bytes 65568 | tf_op jit(solution)/shard_map/ppermute | solution.py:207
  99.4 6.0 %stage.12 = (f32[64,32,128]{2,1,0:T(8,128)S(1)}, f32[4,32,128]{2,1,0:T(8,128)}, f32[4,32,128]{2,1,0:T(8,128)}) custom-call(s32[5]{0:T(128)S(1)} %stack.79.place, s32[1,94]{1,0:T(1,128)S(1)} %copy-done.3, s32[1,94]{1,0:T(1,128)S(1)} %copy-done.4, s32[1,94]{1,0:T(1,128)S(1)} %collective-permute-done.other_rows.refs_3_, ...), custom_call_target="tpu_custom_call" | custom-call | tf_op jit(solution)/shard_map/stage/pallas_call | solution.py:149
  105.3 14.5 %all_to_all.44.refs_5_ = f32[16,4,32,128]{3,2,1,0:T(8,128)S(1)} all-to-all(f32[16,4,32,128]{3,2,1,0:T(8,128)S(1)} %bitcast.30), channel_id=1, replica_groups=mesh['chain'=8,'col'=16] {'col'}, dimensions={0} | all-to-all | bytes 2097152 | tf_op jit(solution)/shard_map/all_to_all | solution.py:172
  119.9 2.6 %stage.13 = (f32[64,32,128]{2,1,0:T(8,128)S(1)}, f32[4,32,128]{2,1,0:T(8,128)}, f32[4,32,128]{2,1,0:T(8,128)}) custom-call(s32[5]{0:T(128)S(1)} %stack.83.refs_0_, s32[1,94]{1,0:T(1,128)S(1)} %copy-done.3, s32[1,94]{1,0:T(1,128)S(1)} %copy-done.4, s32[1,94]{1,0:T(1,128)S(1)} %collective-permute-done.other_rows.refs_3_, ...), custom_call_target="tpu_custom_call" | custom-call | tf_op jit(solution)/shard_map/stage/pallas_call | solution.py:149
  122.5 14.5 %all_to_all.45.arrived = f32[16,4,32,128]{3,2,1,0:T(8,128)S(1)} all-to-all(f32[16,4,32,128]{3,2,1,0:T(8,128)S(1)} %bitcast.34), channel_id=1, replica_groups=mesh['chain'=8,'col'=16] {'col'}, dimensions={0} | all-to-all | bytes 2097152 | tf_op jit(solution)/shard_map/all_to_all | solution.py:172
  137.0 0.1 gather_sum.6
  137.0 0.2 collective-permute-start.7
  137.2 3.3 %collective-permute-done.7 = f32[4,32,128]{2,1,0:T(8,128)S(1)} collective-permute-done((f32[4,32,128]{2,1,0:T(8,128)S(1)}, f32[4,32,128]{2,1,0:T(8,128)S(1)}, u32[]{:S(2)}, u32[]{:S(2)}) %collective-permute-start.7) | collective-permute-done | bytes 65568 | tf_op jit(solution)/shard_map/ppermute | solution.py:207
  140.5 2.6 %stage.14 = (f32[64,32,128]{2,1,0:T(8,128)S(1)}, f32[4,32,128]{2,1,0:T(8,128)S(1)}, f32[4,32,128]{2,1,0:T(8,128)}) custom-call(s32[5]{0:T(128)S(1)} %stack.81.place, s32[1,94]{1,0:T(1,128)S(1)} %copy-done.3, s32[1,94]{1,0:T(1,128)S(1)} %copy-done.4, s32[1,94]{1,0:T(1,128)S(1)} %collective-permute-done.other_rows.refs_3_, ...), custom_call_target="tpu_custom_call" | custom-call | tf_op jit(solution)/shard_map/stage/pallas_call | solution.py:149
  143.1 14.5 %all_to_all.46.refs_5_ = f32[16,4,32,128]{3,2,1,0:T(8,128)S(1)} all-to-all(f32[16,4,32,128]{3,2,1,0:T(8,128)S(1)} %bitcast.28), channel_id=1, replica_groups=mesh['chain'=8,'col'=16] {'col'}, dimensions={0} | all-to-all | bytes 2097152 | tf_op jit(solution)/shard_map/all_to_all | solution.py:172
  157.6 2.1 %stage.15 = (f32[64,32,128]{2,1,0:T(8,128)S(1)}, f32[4,32,128]{2,1,0:T(8,128)S(1)}, f32[4,32,128]{2,1,0:T(8,128)S(1)}) custom-call(s32[5]{0:T(128)S(1)} %stack.83.refs_0_, s32[1,94]{1,0:T(1,128)S(1)} %copy-done.3, s32[1,94]{1,0:T(1,128)S(1)} %copy-done.4, s32[1,94]{1,0:T(1,128)S(1)} %collective-permute-done.other_rows.refs_3_, ...), custom_call_target="tpu_custom_call" | custom-call | tf_op jit(solution)/shard_map/stage/pallas_call | solution.py:149
  159.7 14.5 %all_to_all.47.arrived = f32[16,4,32,128]{3,2,1,0:T(8,128)S(1)} all-to-all(f32[16,4,32,128]{3,2,1,0:T(8,128)S(1)} %bitcast.27), channel_id=1, replica_groups=mesh['chain'=8,'col'=16] {'col'}, dimensions={0} | all-to-all | bytes 2097152 | tf_op jit(solution)/shard_map/all_to_all | solution.py:172
  174.1 0.1 gather_sum.7
  174.2 12.7 %collective-permute-start.8 = (f32[2,4,32,128]{3,2,1,0:T(8,128)S(1)}, f32[2,4,32,128]{3,2,1,0:T(8,128)S(1)}, u32[]{:S(2)}, u32[]{:S(2)}) collective-permute-start(f32[2,4,32,128]{3,2,1,0:T(8,128)S(1)} %get-tuple-element.47), channel_id=1, source_target_pairs={{0,16},{16,0},{32,48},{48,32},{64,80},{80,64},{96,112},{112,96},{1... | collective-permute-start | bytes 393224 | tf_op jit(solution)/shard_map/ppermute | solution.py:169
  186.9 1.0 collective-permute-done.8
  187.9 0.7 fusion.2
  (11 shorter events, 0.1 us)
Async XLA Ops:
  1.1 11.6 %collective-permute-start.3 = (f32[94,128,128]{2,1,0:T(8,128)}, f32[94,128,128]{2,1,0:T(8,128)S(1)}, u32[]{:S(2)}, u32[]{:S(2)}) collective-permute-start(f32[94,128,128]{2,1,0:T(8,128)} %bitcast.25), channel_id=1, source_target_pairs={{0,16},{16,0},{32,48},{48,32},{64,80},{80,64},{96,112},{112,96},{1... | collective-permute-start | bytes 18481160 | tf_op jit(solution)/shard_map/ppermute | solution.py:169
  2.5 12.0 %copy-start.3 = (s32[1,94]{1,0:T(1,128)S(1)}, s32[1,94]{1,0:T(1,128)}, u32[]{:S(2)}) copy-start(s32[1,94]{1,0:T(1,128)} %refs_1_.7) | copy-start | bytes 1132
  2.5 12.0 %copy-start.4 = (s32[1,94]{1,0:T(1,128)S(1)}, s32[1,94]{1,0:T(1,128)}, u32[]{:S(2)}) copy-start(s32[1,94]{1,0:T(1,128)} %refs_2_.7) | copy-start | bytes 1132
  2.5 12.0 %copy-start = (f32[1,4,64,128]{3,2,1,0:T(8,128)S(1)}, f32[1,4,64,128]{3,2,1,0:T(8,128)}, u32[]{:S(2)}) copy-start(f32[1,4,64,128]{3,2,1,0:T(8,128)} %refs_6_.7) | copy-start | bytes 393220
  2.5 10.2 %collective-permute-start.4 = (f32[4,128,128]{2,1,0:T(8,128)}, f32[4,128,128]{2,1,0:T(8,128)S(1)}, u32[]{:S(2)}, u32[]{:S(2)}) collective-permute-start(f32[4,128,128]{2,1,0:T(8,128)} %bitcast.39), channel_id=1, source_target_pairs={{0,16},{16,0},{32,48},{48,32},{64,80},{80,64},{96,112},{112,96},{1... | collective-permute-start | bytes 786440 | tf_op jit(solution)/shard_map/ppermute | solution.py:169
  2.6 11.8 %collective-permute-start.2 = (f32[1,4,64,128]{3,2,1,0:T(8,128)}, f32[1,4,64,128]{3,2,1,0:T(8,128)S(1)}, u32[]{:S(2)}, u32[]{:S(2)}) collective-permute-start(f32[1,4,64,128]{3,2,1,0:T(8,128)} %refs_6_.7), channel_id=1, source_target_pairs={{0,16},{16,0},{32,48},{48,32},{64,80},{80,64},{96,112},{112,96},{1... | collective-permute-start | bytes 393224 | tf_op jit(solution)/shard_map/ppermute | solution.py:169
  3.0 11.4 %collective-permute-start = (s32[1,94]{1,0:T(1,128)}, s32[1,94]{1,0:T(1,128)S(1)}, u32[]{:S(2)}, u32[]{:S(2)}) collective-permute-start(s32[1,94]{1,0:T(1,128)} %refs_1_.7), channel_id=1, source_target_pairs={{0,16},{16,0},{32,48},{48,32},{64,80},{80,64},{96,112},{112,96},{1... | collective-permute-start | bytes 1136 | tf_op jit(solution)/shard_map/ppermute | solution.py:169
  3.1 11.3 %collective-permute-start.1 = (s32[1,94]{1,0:T(1,128)}, s32[1,94]{1,0:T(1,128)S(1)}, u32[]{:S(2)}, u32[]{:S(2)}) collective-permute-start(s32[1,94]{1,0:T(1,128)} %refs_2_.7), channel_id=1, source_target_pairs={{0,16},{16,0},{32,48},{48,32},{64,80},{80,64},{96,112},{112,96},{1... | collective-permute-start | bytes 1136 | tf_op jit(solution)/shard_map/ppermute | solution.py:169
  3.5 2.7 %copy-start.1 = (f32[1,94,128,128]{3,2,1,0:T(8,128)S(1)}, f32[1,94,128,128]{3,2,1,0:T(8,128)}, u32[]{:S(2)}) copy-start(f32[1,94,128,128]{3,2,1,0:T(8,128)} %param.7) | copy-start | bytes 18481156
  6.3 0.9 copy-start.2
  56.7 3.5 %collective-permute-start.5 = (f32[4,32,128]{2,1,0:T(8,128)S(1)}, f32[4,32,128]{2,1,0:T(8,128)S(1)}, u32[]{:S(2)}, u32[]{:S(2)}) collective-permute-start(f32[4,32,128]{2,1,0:T(8,128)S(1)} %gather_sum.4), channel_id=1, source_target_pairs={{0,32},{16,48},{32,0},{48,16},{64,96},{80,112},{96,64},{112,80},{1... | collective-permute-start | bytes 196616 | tf_op jit(solution)/shard_map/ppermute | solution.py:207
  94.6 4.8 %collective-permute-start.6 = (f32[4,32,128]{2,1,0:T(8,128)S(1)}, f32[4,32,128]{2,1,0:T(8,128)S(1)}, u32[]{:S(2)}, u32[]{:S(2)}) collective-permute-start(f32[4,32,128]{2,1,0:T(8,128)S(1)} %gather_sum.5), channel_id=1, source_target_pairs={{0,96},{16,112},{32,64},{48,80},{64,32},{80,48},{96,0},{112,16},{1... | collective-permute-start | bytes 196616 | tf_op jit(solution)/shard_map/ppermute | solution.py:207
  137.0 3.5 %collective-permute-start.7 = (f32[4,32,128]{2,1,0:T(8,128)S(1)}, f32[4,32,128]{2,1,0:T(8,128)S(1)}, u32[]{:S(2)}, u32[]{:S(2)}) collective-permute-start(f32[4,32,128]{2,1,0:T(8,128)S(1)} %gather_sum.6), channel_id=1, source_target_pairs={{0,32},{16,48},{32,0},{48,16},{64,96},{80,112},{96,64},{112,80},{1... | collective-permute-start | bytes 196616 | tf_op jit(solution)/shard_map/ppermute | solution.py:207
  174.2 13.7 %collective-permute-start.8 = (f32[2,4,32,128]{3,2,1,0:T(8,128)S(1)}, f32[2,4,32,128]{3,2,1,0:T(8,128)S(1)}, u32[]{:S(2)}, u32[]{:S(2)}) collective-permute-start(f32[2,4,32,128]{3,2,1,0:T(8,128)S(1)} %get-tuple-element.47), channel_id=1, source_target_pairs={{0,16},{16,0},{32,48},{48,32},{64,80},{80,64},{96,112},{112,96},{1... | collective-permute-start | bytes 393224 | tf_op jit(solution)/shard_map/ppermute | solution.py:169

commit v5 on v4

--- a/solution.py
+++ b/solution.py
@@ -49,42 +49,26 @@
         prepare_tile(tile_ref[i], out_ref, first + i)
 
 
-def prepare_own_body(tile_ref, inverse_ref, out_ref, out_inverse_ref):
+def prepare_own_body(tile_ref, inverse_ref, *refs):
+    out_ref, out_inverse_ref = refs[-2:]
     prepare_tiles(tile_ref, out_ref, 0, tile_ref.shape[0])
     prepare_tiles(inverse_ref, out_inverse_ref, 0, inverse_ref.shape[0])
 
 
-def prepare_other_body(tile_ref, inverse_ref, held_ref, held_inverse_ref, out_ref, out_inverse_ref):
-    count, columns = tile_ref.shape[0], inverse_ref.shape[0]
-    prepare_tiles(tile_ref, out_ref, count, count)
-    prepare_tiles(inverse_ref, out_inverse_ref, columns, columns)
-
-
-def prepare(own, own_inverse, other, other_inverse):
-    count, size = own.shape[0], own.shape[1]
-    columns = own_inverse.shape[0]
-    shapes = (
-        jax.ShapeDtypeStruct((2 * count, 2 * size, size), BF),
-        jax.ShapeDtypeStruct((2 * columns, 2 * size, size), BF),
-    )
-    grant = pltpu.CompilerParams(vmem_limit_bytes=20 << 20)
-    held = pl.pallas_call(
+def prepare_shapes(own, own_inverse):
+    size = own.shape[1]
+    return tuple(jax.ShapeDtypeStruct((2 * x.shape[0], 2 * size, size), BF) for x in (own, own_inverse))
+
+
+def prepare_own(own, own_inverse, sources, tables):
+    return pl.pallas_call(
         prepare_own_body,
-        out_shape=shapes,
-        in_specs=[VMEM, VMEM],
+        out_shape=prepare_shapes(own, own_inverse),
+        in_specs=[VMEM, VMEM, VMEM, SMEM, SMEM],
         out_specs=(VMEM, VMEM),
-        compiler_params=grant,
+        compiler_params=pltpu.CompilerParams(vmem_limit_bytes=20 << 20),
         name="prepare_own",
-    )(own, own_inverse)
-    return pl.pallas_call(
-        prepare_other_body,
-        out_shape=shapes,
-        in_specs=[VMEM] * 4,
-        out_specs=(VMEM, VMEM),
-        input_output_aliases={2: 0, 3: 1},
-        compiler_params=grant,
-        name="prepare_other",
-    )(other, other_inverse, *held)
+    )(own, own_inverse, sources, *tables)
 
 
 def gather_sum_body(arrived, total):
@@ -106,48 +90,87 @@
     )(arrived)
 
 
-def stage_body(
-    place, rows, cols, other_rows, other_cols, arrived, before, source, other_source, inverse, factor, sums, solved, inbound, current
-):
-    slot, origin, first, shift = place[0], place[1], place[2], place[3]
+def rates(place, k, rows, cols, other_rows, other_cols):
+    other = place[0] > 0
+    row = jnp.where(other, other_rows[0, k], rows[0, k])
+    return row, jnp.where(other, other_cols[0, k], cols[0, k]) - place[3]
+
+
+def clear(sums, times):
+    if times is None:
+        sums[...] = jnp.zeros_like(sums)
+    else:
+
+        @pl.loop(0, times)
+        def _(_):
+            sums[...] = jnp.zeros_like(sums)
+
+
+def sources_of(place, t, width, source, other_source):
+    here = pl.ds(pl.multiple_of(place[2], width), width)
+    return jnp.where(place[0] > 0, other_source[0, t, here], source[0, t, here])
+
+
+def opening_body(place, *refs):
+    tables, refs = refs[:4], refs[4:]
+    source, other_source, tile_ref, tile_inverse_ref, _, _, sums, factor, inverse, current = refs
+    tiles, columns, width = tile_ref.shape[0], tile_inverse_ref.shape[0], sums.shape[1]
+    prepare_tiles(tile_inverse_ref, inverse, columns, columns)
+    clear(sums, place[4])
+    for t in range(columns):
+        right = sources_of(place, t, width, source, other_source)
+        current[t] = left_side(product(left_side(right), inverse[place[0] * columns + t]))
+    for k in range(tiles):
+        prepare_tile(tile_ref[k], factor, tiles + k)
+        row, col = rates(place, k, *tables)
+        sums[row] += product(current[col], factor[place[0] * tiles + k])
+
+
+def opening(place, tables, sources, other_sources, other, other_inverse, held, tile_rows):
+    _, columns, width, size = sources.shape
+    width = width // 2
+    return pl.pallas_call(
+        opening_body,
+        out_shape=(jax.ShapeDtypeStruct((tile_rows, width, size), F32),) + prepare_shapes(other, other_inverse),
+        in_specs=[SMEM] * 5 + [VMEM] * 6,
+        out_specs=(VMEM,) * 3,
+        scratch_shapes=[pltpu.VMEM((columns, 2 * width, 2 * size), BF)],
+        input_output_aliases={9: 1, 10: 2},
+        compiler_params=pltpu.CompilerParams(vmem_limit_bytes=20 << 20),
+        name="opening",
+    )(place, *tables, sources, other_sources, other, other_inverse, *held)
+
+
+def stage_body(paced, place, *refs):
+    tables, refs = refs[:4], refs[4:]
+    arrived, refs = refs[0], refs[1:]
+    before, refs = (refs[0], refs[1:]) if len(refs) == 9 else (None, refs)
+    source, other_source, inverse, factor, sums, solved, inbound, current = refs
     tiles = factor.shape[0] // 2
     columns, width = inbound.shape[0], inbound.shape[1]
-    here = pl.ds(pl.multiple_of(first, width), width)
-
-    @pl.loop(0, place[4])
-    def _(_):
-        sums[...] = jnp.zeros_like(sums)
-
+    clear(sums, place[4] if paced else None)
     for t in range(columns):
         total = arrived[0, t]
         for j in range(1, arrived.shape[0]):
             total = total + arrived[j, t]
         if before is not None:
-            total = jnp.where(origin == NEW, total, jnp.where(origin == OLD, before[0, t], jnp.zeros_like(total)))
+            kept = jnp.where(place[1] == OLD, before[0, t], jnp.zeros_like(total))
+            total = jnp.where(place[1] == NEW, total, kept)
         inbound[t] = total
-        right = jnp.where(slot > 0, other_source[0, t, here], source[0, t, here]) - total
-        value = product(left_side(right), inverse[slot * columns + t])
+        right = sources_of(place, t, width, source, other_source) - total
+        value = product(left_side(right), inverse[place[0] * columns + t])
         solved[t] = value
         current[t] = left_side(value)
-    base = slot * tiles
     for k in range(tiles):
-        row = jnp.where(slot > 0, other_rows[0, k], rows[0, k])
-        col = jnp.where(slot > 0, other_cols[0, k], cols[0, k]) - shift
-        sums[row] += product(current[col], factor[base + k])
-
-
-def stage(place, tables, arrived, before, inputs, tile_rows):
-    body = stage_body
-    if before is None:
-
-        def body(*refs):
-            stage_body(*refs[:6], None, *refs[6:])
-
-    arrivals = (arrived,) if before is None else (arrived, before)
-    small = jax.ShapeDtypeStruct(arrived.shape[1:], F32)
+        row, col = rates(place, k, *tables)
+        sums[row] += product(current[col], factor[place[0] * tiles + k])
+
+
+def stage(place, tables, arrivals, inputs, tile_rows, paced=False):
+    small = jax.ShapeDtypeStruct(arrivals[0].shape[1:], F32)
     columns, width, size = small.shape
     return pl.pallas_call(
-        body,
+        functools.partial(stage_body, paced),
         out_shape=(jax.ShapeDtypeStruct((tile_rows, width, size), F32), small, small),
         in_specs=[SMEM] * 5 + [VMEM] * (len(arrivals) + 4),
         out_specs=[VMEM, VMEM, VMEM],
@@ -190,16 +213,21 @@
     tables = (tile_rows, tile_cols, swap(tile_rows), swap(tile_cols))
     other_sources = swap(sources)
     other_factor = swap(factor_tiles[0])
-    factor, inverse = prepare(factor_tiles[0], diag_inverse[0], other_factor, other_inverse)
+    held = prepare_own(factor_tiles[0], diag_inverse[0], sources, tables[:2])
+    tile_total = peers * columns
+    sums, factor, inverse = opening(
+        place[0], tables, sources, other_sources, other_factor, other_inverse, held, tile_total
+    )
     inputs = (sources, other_sources, inverse, factor)
 
     trades = [{0: 1, 1: 0, 2: 3, 3: 2}, {0: 3, 1: 2, 2: 1, 3: 0}, {0: 1, 1: 0, 2: 3, 3: 2}]
-    arrived = jnp.zeros((1, columns, width, sources.shape[3]), F32)
-    before = arrived
+    arrived = before = None
     planes = groups // 2
     for sweep in range(planes):
-        sums, solved_even, _ = stage(place[sweep], tables, arrived, before, inputs, peers * columns)
-        sums, solved_odd, leaving_even = stage(place[-1], tables, exchange(sums), None, inputs, peers * columns)
+        if sweep:
+            arrivals = (arrived, arrived if before is None else before)
+            sums, solved_even, _ = stage(place[sweep], tables, arrivals, inputs, tile_total, paced=sweep == 2)
+        sums, solved_odd, leaving_even = stage(place[-1], tables, (exchange(sums),), inputs, tile_total)
         leaving_odd = gather_sum(exchange(sums))
         if sweep < planes - 1:
             trade = trades[sweep]

time: 189 us -> 188 us (level)
  waiting for transfers between devices: 12.1 us -> 9.6 us
  local copies, waits for them, and re-layouts: 4.85 us -> 7.05 us
    ppermute x6, waiting for transfers between devices: 4.73 us -> 2.16 us  [swap(): return lax.ppermute(x, 'chain', [(i, i ^ 1) for i in range(groups)])]
    unnamed x10, local copies, waits for them, and re-layouts: 3.71 us -> 5.91 us
    pallas_call x10 -> x9, Pallas kernels: 27.2 us -> 26.6 us  [the longest x7 21.2 us: stage(): pl.pallas_call(functools.partial(stage_body, paced), out_shape=(jax.Shape...]
  transfers between devices with their start and end apart: 9 -> 9, of which waited for: 5 -> 5; matrix products, arithmetic and copies ran while one was open for 0% -> 0% of each run, Pallas kernels for 2% -> 1%
where the time goes in v5:
time: 188 us
  blocking collectives  124 us (66%)
  Pallas kernels  26.8 us (14%)
  starting transfers between devices  19.4 us (10%)
  waiting for transfers between devices  9.6 us (5%)
  local copies, waits for them, and re-layouts  7.05 us (4%)
    all_to_all x8, blocking collectives, exchange(): lax.all_to_all(x.reshape((peers, columns) + x.shape[1:]), 'col', 0, 0)  124 us
    pallas_call x7, Pallas kernels, stage(): pl.pallas_call(functools.partial(stage_body, paced), out_shape=(jax.Shape...  21.2 us
    ppermute x6, starting transfers between devices, swap(): return lax.ppermute(x, 'chain', [(i, i ^ 1) for i in range(groups)])  15.1 us
    ppermute x3, waiting for transfers between devices, local(): before, arrived = (arrived, lax.ppermute(leaving_odd, 'chain', route)[None])  7.43 us
    unnamed x10, local copies, waits for them, and re-layouts  5.91 us
    ppermute x3, starting transfers between devices, local(): before, arrived = (arrived, lax.ppermute(leaving_odd, 'chain', route)[None])  4.29 us
  transfers between devices with their start and end apart: 9, of which 5 were waited for; matrix products, arithmetic and copies ran while one was open for 0% of the time, Pallas kernels for 1%

profile of v5, /device:TPU:1, one launch (start us, length us, event | category | flops | bytes accessed | tf_op | source)
XLA Modules:
  0.0 187.6 jit_solution(3056151284179682412)
XLA Ops:
  0.7 0.1 stack.76.place
  0.8 0.1 stack.79.place
  0.8 0.1 stack.77.place
  0.9 0.1 stack.81.place
  1.0 0.1 stack.83.place
  1.1 1.4 collective-permute-start.3
  2.5 0.1 collective-permute-start.4
  2.6 0.4 collective-permute-start.2
  3.0 0.1 collective-permute-start
  3.1 0.4 collective-permute-start.1
  3.5 0.9 copy-done
  4.4 2.7 %copy-done.1 = f32[1,94,128,128]{3,2,1,0:T(8,128)S(1)} copy-done((f32[1,94,128,128]{3,2,1,0:T(8,128)S(1)}, f32[1,94,128,128]{3,2,1,0:T(8,128)}, u32[]{:S(2)}) %copy-start.1) | copy-done | bytes 6160408
  7.2 0.9 copy-done.2
  8.1 0.7 copy-done.3
  8.8 0.7 copy-done.4
  9.4 2.3 %prepare_own.1 = (bf16[188,256,128]{2,1,0:T(8,128)(2,1)S(1)}, bf16[8,256,128]{2,1,0:T(8,128)(2,1)S(1)}) custom-call(f32[94,128,128]{2,1,0:T(8,128)S(1)} %bitcast.26, f32[4,128,128]{2,1,0:T(8,128)S(1)} %bitcast.41, f32[1,4,64,128]{3,2,1,0:T(8,128)S(1)} %copy-done, s32[1,94]{1,0:T(1,128)S(1)} %copy-done.3, s32[1,94]{1,0:T(1,128)S(1)} %copy-done.4), custom_call_target="tpu_custom_call" | custom-call | tf_op jit(solution)/shard_map/prepare_own/pallas_call | solution.py:64
  11.7 1.2 collective-permute-done.refs_2_
  12.9 0.0 collective-permute-done.1.refs_3_
  12.9 0.0 collective-permute-done.2.refs_5_.refs_6_.refs_7_
  12.9 3.2 %opening.1 = (f32[64,32,128]{2,1,0:T(8,128)S(1)}, bf16[188,256,128]{2,1,0:T(8,128)(2,1)S(1)}, bf16[8,256,128]{2,1,0:T(8,128)(2,1)S(1)}) custom-call(s32[5]{0:T(128)S(1)} %stack.76.place, s32[1,94]{1,0:T(1,128)S(1)} %copy-done.3, s32[1,94]{1,0:T(1,128)S(1)} %copy-done.4, ...), custom_call_target="tpu_custom_call", output_to_operand_aliasing={{1}: (9, {}), {2}: (10, {})} | custom-call | tf_op jit(solution)/shard_map/opening/pallas_call | solution.py:132
  16.1 20.8 %all_to_all.40.refs_4_ = f32[16,4,32,128]{3,2,1,0:T(8,128)S(1)} all-to-all(f32[16,4,32,128]{3,2,1,0:T(8,128)S(1)} %bitcast.28), channel_id=1, replica_groups=mesh['chain'=8,'col'=16] {'col'}, dimensions={0} | all-to-all | bytes 2097152 | tf_op jit(solution)/shard_map/all_to_all | solution.py:195
  36.8 2.6 %stage.7 = (f32[64,32,128]{2,1,0:T(8,128)S(1)}, f32[4,32,128]{2,1,0:T(8,128)}, f32[4,32,128]{2,1,0:T(8,128)}) custom-call(s32[5]{0:T(128)S(1)} %stack.83.place, s32[1,94]{1,0:T(1,128)S(1)} %copy-done.3, s32[1,94]{1,0:T(1,128)S(1)} %copy-done.4, s32[1,94]{1,0:T(1,128)S(1)} %collective-permute-done.refs_2_, s32[1,94]{1,0:T(1,128)S(1)} %collective-permute-done.1.refs_3_, ...), custom_call_target="tpu_custom_call" | custom-call | tf_op jit(solution)/shard_map/stage/pallas_call | solution.py:172
  39.4 16.2 %all_to_all.41.arrived = f32[16,4,32,128]{3,2,1,0:T(8,128)S(1)} all-to-all(f32[16,4,32,128]{3,2,1,0:T(8,128)S(1)} %bitcast.31), channel_id=1, replica_groups=mesh['chain'=8,'col'=16] {'col'}, dimensions={0} | all-to-all | bytes 2097152 | tf_op jit(solution)/shard_map/all_to_all | solution.py:195
  55.6 0.1 gather_sum.4
  55.6 1.4 collective-permute-start.5
  57.0 2.1 %collective-permute-done.5 = f32[4,32,128]{2,1,0:T(8,128)S(1)} collective-permute-done((f32[4,32,128]{2,1,0:T(8,128)S(1)}, f32[4,32,128]{2,1,0:T(8,128)S(1)}, u32[]{:S(2)}, u32[]{:S(2)}) %collective-permute-start.5) | collective-permute-done | bytes 65568 | tf_op jit(solution)/shard_map/ppermute | solution.py:235
  59.1 2.6 %stage.8 = (f32[64,32,128]{2,1,0:T(8,128)S(1)}, f32[4,32,128]{2,1,0:T(8,128)}, f32[4,32,128]{2,1,0:T(8,128)}) custom-call(s32[5]{0:T(128)S(1)} %stack.77.place, s32[1,94]{1,0:T(1,128)S(1)} %copy-done.3, s32[1,94]{1,0:T(1,128)S(1)} %copy-done.4, s32[1,94]{1,0:T(1,128)S(1)} %collective-permute-done.refs_2_, s32[1,94]{1,0:T(1,128)S(1)} %collective-permute-done.1.refs_3_, ...), custom_call_target="tpu_custom_call" | custom-call | tf_op jit(solution)/shard_map/stage/pallas_call | solution.py:172
  61.7 14.5 %all_to_all.42.refs_4_ = f32[16,4,32,128]{3,2,1,0:T(8,128)S(1)} all-to-all(f32[16,4,32,128]{3,2,1,0:T(8,128)S(1)} %bitcast.32), channel_id=1, replica_groups=mesh['chain'=8,'col'=16] {'col'}, dimensions={0} | all-to-all | bytes 2097152 | tf_op jit(solution)/shard_map/all_to_all | solution.py:195
  76.2 2.6 %stage.9 = (f32[64,32,128]{2,1,0:T(8,128)S(1)}, f32[4,32,128]{2,1,0:T(8,128)}, f32[4,32,128]{2,1,0:T(8,128)}) custom-call(s32[5]{0:T(128)S(1)} %stack.83.place, s32[1,94]{1,0:T(1,128)S(1)} %copy-done.3, s32[1,94]{1,0:T(1,128)S(1)} %copy-done.4, s32[1,94]{1,0:T(1,128)S(1)} %collective-permute-done.refs_2_, s32[1,94]{1,0:T(1,128)S(1)} %collective-permute-done.1.refs_3_, ...), custom_call_target="tpu_custom_call" | custom-call | tf_op jit(solution)/shard_map/stage/pallas_call | solution.py:172
  78.8 14.5 %all_to_all.43.arrived = f32[16,4,32,128]{3,2,1,0:T(8,128)S(1)} all-to-all(f32[16,4,32,128]{3,2,1,0:T(8,128)S(1)} %bitcast.33), channel_id=1, replica_groups=mesh['chain'=8,'col'=16] {'col'}, dimensions={0} | all-to-all | bytes 2097152 | tf_op jit(solution)/shard_map/all_to_all | solution.py:195
  93.3 0.1 gather_sum.5
  93.3 2.8 %collective-permute-start.6 = (f32[4,32,128]{2,1,0:T(8,128)S(1)}, f32[4,32,128]{2,1,0:T(8,128)S(1)}, u32[]{:S(2)}, u32[]{:S(2)}) collective-permute-start(f32[4,32,128]{2,1,0:T(8,128)S(1)} %gather_sum.5), channel_id=1, source_target_pairs={{0,96},{16,112},{32,64},{48,80},{64,32},{80,48},{96,0},{112,16},{1... | collective-permute-start | bytes 196616 | tf_op jit(solution)/shard_map/ppermute | solution.py:235
  96.1 2.0 %collective-permute-done.6 = f32[4,32,128]{2,1,0:T(8,128)S(1)} collective-permute-done((f32[4,32,128]{2,1,0:T(8,128)S(1)}, f32[4,32,128]{2,1,0:T(8,128)S(1)}, u32[]{:S(2)}, u32[]{:S(2)}) %collective-permute-start.6) | collective-permute-done | bytes 65568 | tf_op jit(solution)/shard_map/ppermute | solution.py:235
  98.1 6.2 %stage.10 = (f32[64,32,128]{2,1,0:T(8,128)S(1)}, f32[4,32,128]{2,1,0:T(8,128)}, f32[4,32,128]{2,1,0:T(8,128)}) custom-call(s32[5]{0:T(128)S(1)} %stack.79.place, s32[1,94]{1,0:T(1,128)S(1)} %copy-done.3, s32[1,94]{1,0:T(1,128)S(1)} %copy-done.4, s32[1,94]{1,0:T(1,128)S(1)} %collective-permute-done.refs_2_, s32[1,94]{1,0:T(1,128)S(1)} %collective-permute-done.1.refs_3_, ...), custom_call_target="tpu_custom_call" | custom-call | tf_op jit(solution)/shard_map/stage/pallas_call | solution.py:172
  104.2 14.7 %all_to_all.44.refs_4_ = f32[16,4,32,128]{3,2,1,0:T(8,128)S(1)} all-to-all(f32[16,4,32,128]{3,2,1,0:T(8,128)S(1)} %bitcast.30), channel_id=1, replica_groups=mesh['chain'=8,'col'=16] {'col'}, dimensions={0} | all-to-all | bytes 2097152 | tf_op jit(solution)/shard_map/all_to_all | solution.py:195
  119.0 2.6 %stage.11 = (f32[64,32,128]{2,1,0:T(8,128)S(1)}, f32[4,32,128]{2,1,0:T(8,128)}, f32[4,32,128]{2,1,0:T(8,128)}) custom-call(s32[5]{0:T(128)S(1)} %stack.83.place, s32[1,94]{1,0:T(1,128)S(1)} %copy-done.3, s32[1,94]{1,0:T(1,128)S(1)} %copy-done.4, s32[1,94]{1,0:T(1,128)S(1)} %collective-permute-done.refs_2_, s32[1,94]{1,0:T(1,128)S(1)} %collective-permute-done.1.refs_3_, ...), custom_call_target="tpu_custom_call" | custom-call | tf_op jit(solution)/shard_map/stage/pallas_call | solution.py:172
  121.6 14.5 %all_to_all.45.arrived = f32[16,4,32,128]{3,2,1,0:T(8,128)S(1)} all-to-all(f32[16,4,32,128]{3,2,1,0:T(8,128)S(1)} %bitcast.34), channel_id=1, replica_groups=mesh['chain'=8,'col'=16] {'col'}, dimensions={0} | all-to-all | bytes 2097152 | tf_op jit(solution)/shard_map/all_to_all | solution.py:195
  136.0 0.1 gather_sum.6
  136.1 0.1 collective-permute-start.7
  136.2 3.4 %collective-permute-done.7 = f32[4,32,128]{2,1,0:T(8,128)S(1)} collective-permute-done((f32[4,32,128]{2,1,0:T(8,128)S(1)}, f32[4,32,128]{2,1,0:T(8,128)S(1)}, u32[]{:S(2)}, u32[]{:S(2)}) %collective-permute-start.7) | collective-permute-done | bytes 65568 | tf_op jit(solution)/shard_map/ppermute | solution.py:235
  139.6 2.6 %stage.12 = (f32[64,32,128]{2,1,0:T(8,128)S(1)}, f32[4,32,128]{2,1,0:T(8,128)S(1)}, f32[4,32,128]{2,1,0:T(8,128)}) custom-call(s32[5]{0:T(128)S(1)} %stack.81.place, s32[1,94]{1,0:T(1,128)S(1)} %copy-done.3, s32[1,94]{1,0:T(1,128)S(1)} %copy-done.4, s32[1,94]{1,0:T(1,128)S(1)} %collective-permute-done.refs_2_, s32[1,94]{1,0:T(1,128)S(1)} %collective-permute-done.1.refs_3_, ...), custom_call_target="tpu_custom_call" | custom-call | tf_op jit(solution)/shard_map/stage/pallas_call | solution.py:172
  142.2 14.5 %all_to_all.46.refs_4_ = f32[16,4,32,128]{3,2,1,0:T(8,128)S(1)} all-to-all(f32[16,4,32,128]{3,2,1,0:T(8,128)S(1)} %bitcast.29), channel_id=1, replica_groups=mesh['chain'=8,'col'=16] {'col'}, dimensions={0} | all-to-all | bytes 2097152 | tf_op jit(solution)/shard_map/all_to_all | solution.py:195
  156.6 2.0 %stage.13 = (f32[64,32,128]{2,1,0:T(8,128)S(1)}, f32[4,32,128]{2,1,0:T(8,128)S(1)}, f32[4,32,128]{2,1,0:T(8,128)S(1)}) custom-call(s32[5]{0:T(128)S(1)} %stack.83.place, s32[1,94]{1,0:T(1,128)S(1)} %copy-done.3, s32[1,94]{1,0:T(1,128)S(1)} %copy-done.4, s32[1,94]{1,0:T(1,128)S(1)} %collective-permute-done.refs_2_, ...), custom_call_target="tpu_custom_call" | custom-call | tf_op jit(solution)/shard_map/stage/pallas_call | solution.py:172
  158.7 14.5 %all_to_all.47.arrived = f32[16,4,32,128]{3,2,1,0:T(8,128)S(1)} all-to-all(f32[16,4,32,128]{3,2,1,0:T(8,128)S(1)} %bitcast.27), channel_id=1, replica_groups=mesh['chain'=8,'col'=16] {'col'}, dimensions={0} | all-to-all | bytes 2097152 | tf_op jit(solution)/shard_map/all_to_all | solution.py:195
  173.1 0.1 gather_sum.7
  173.2 12.7 %collective-permute-start.8 = (f32[2,4,32,128]{3,2,1,0:T(8,128)S(1)}, f32[2,4,32,128]{3,2,1,0:T(8,128)S(1)}, u32[]{:S(2)}, u32[]{:S(2)}) collective-permute-start(f32[2,4,32,128]{3,2,1,0:T(8,128)S(1)} %get-tuple-element.47), channel_id=1, source_target_pairs={{0,16},{16,0},{32,48},{48,32},{64,80},{80,64},{96,112},{112,96},{1... | collective-permute-start | bytes 393224 | tf_op jit(solution)/shard_map/ppermute | solution.py:192
  185.9 1.0 collective-permute-done.8
  186.9 0.7 fusion.2
  (9 shorter events, 0.1 us)
Async XLA Ops:
  1.1 11.8 %collective-permute-start.3 = (f32[94,128,128]{2,1,0:T(8,128)}, f32[94,128,128]{2,1,0:T(8,128)S(1)}, u32[]{:S(2)}, u32[]{:S(2)}) collective-permute-start(f32[94,128,128]{2,1,0:T(8,128)} %bitcast.25), channel_id=1, source_target_pairs={{0,16},{16,0},{32,48},{48,32},{64,80},{80,64},{96,112},{112,96},{1... | collective-permute-start | bytes 18481160 | tf_op jit(solution)/shard_map/ppermute | solution.py:192
  2.5 10.4 %collective-permute-start.4 = (f32[4,128,128]{2,1,0:T(8,128)}, f32[4,128,128]{2,1,0:T(8,128)S(1)}, u32[]{:S(2)}, u32[]{:S(2)}) collective-permute-start(f32[4,128,128]{2,1,0:T(8,128)} %bitcast.40), channel_id=1, source_target_pairs={{0,16},{16,0},{32,48},{48,32},{64,80},{80,64},{96,112},{112,96},{1... | collective-permute-start | bytes 786440 | tf_op jit(solution)/shard_map/ppermute | solution.py:192
  2.6 10.3 %collective-permute-start.2 = (f32[1,4,64,128]{3,2,1,0:T(8,128)}, f32[1,4,64,128]{3,2,1,0:T(8,128)S(1)}, u32[]{:S(2)}, u32[]{:S(2)}) collective-permute-start(f32[1,4,64,128]{3,2,1,0:T(8,128)} %refs_5_.7), channel_id=1, source_target_pairs={{0,16},{16,0},{32,48},{48,32},{64,80},{80,64},{96,112},{112,96},{1... | collective-permute-start | bytes 393224 | tf_op jit(solution)/shard_map/ppermute | solution.py:192
  3.0 9.9 %collective-permute-start = (s32[1,94]{1,0:T(1,128)}, s32[1,94]{1,0:T(1,128)S(1)}, u32[]{:S(2)}, u32[]{:S(2)}) collective-permute-start(s32[1,94]{1,0:T(1,128)} %refs_0_.17), channel_id=1, source_target_pairs={{0,16},{16,0},{32,48},{48,32},{64,80},{80,64},{96,112},{112,96},{1... | collective-permute-start | bytes 1136 | tf_op jit(solution)/shard_map/ppermute | solution.py:192
  3.1 9.8 %collective-permute-start.1 = (s32[1,94]{1,0:T(1,128)}, s32[1,94]{1,0:T(1,128)S(1)}, u32[]{:S(2)}, u32[]{:S(2)}) collective-permute-start(s32[1,94]{1,0:T(1,128)} %refs_1_.17), channel_id=1, source_target_pairs={{0,16},{16,0},{32,48},{48,32},{64,80},{80,64},{96,112},{112,96},{1... | collective-permute-start | bytes 1136 | tf_op jit(solution)/shard_map/ppermute | solution.py:192
  3.5 0.9 copy-start
  4.4 2.7 %copy-start.1 = (f32[1,94,128,128]{3,2,1,0:T(8,128)S(1)}, f32[1,94,128,128]{3,2,1,0:T(8,128)}, u32[]{:S(2)}) copy-start(f32[1,94,128,128]{3,2,1,0:T(8,128)} %param.7) | copy-start | bytes 18481156
  7.2 0.9 copy-start.2
  8.1 0.7 copy-start.3
  8.8 0.7 copy-start.4
  55.6 3.5 %collective-permute-start.5 = (f32[4,32,128]{2,1,0:T(8,128)S(1)}, f32[4,32,128]{2,1,0:T(8,128)S(1)}, u32[]{:S(2)}, u32[]{:S(2)}) collective-permute-start(f32[4,32,128]{2,1,0:T(8,128)S(1)} %gather_sum.4), channel_id=1, source_target_pairs={{0,32},{16,48},{32,0},{48,16},{64,96},{80,112},{96,64},{112,80},{1... | collective-permute-start | bytes 196616 | tf_op jit(solution)/shard_map/ppermute | solution.py:235
  93.3 4.7 %collective-permute-start.6 = (f32[4,32,128]{2,1,0:T(8,128)S(1)}, f32[4,32,128]{2,1,0:T(8,128)S(1)}, u32[]{:S(2)}, u32[]{:S(2)}) collective-permute-start(f32[4,32,128]{2,1,0:T(8,128)S(1)} %gather_sum.5), channel_id=1, source_target_pairs={{0,96},{16,112},{32,64},{48,80},{64,32},{80,48},{96,0},{112,16},{1... | collective-permute-start | bytes 196616 | tf_op jit(solution)/shard_map/ppermute | solution.py:235
  136.1 3.5 %collective-permute-start.7 = (f32[4,32,128]{2,1,0:T(8,128)S(1)}, f32[4,32,128]{2,1,0:T(8,128)S(1)}, u32[]{:S(2)}, u32[]{:S(2)}) collective-permute-start(f32[4,32,128]{2,1,0:T(8,128)S(1)} %gather_sum.6), channel_id=1, source_target_pairs={{0,32},{16,48},{32,0},{48,16},{64,96},{80,112},{96,64},{112,80},{1... | collective-permute-start | bytes 196616 | tf_op jit(solution)/shard_map/ppermute | solution.py:235
  173.2 13.7 %collective-permute-start.8 = (f32[2,4,32,128]{3,2,1,0:T(8,128)S(1)}, f32[2,4,32,128]{3,2,1,0:T(8,128)S(1)}, u32[]{:S(2)}, u32[]{:S(2)}) collective-permute-start(f32[2,4,32,128]{3,2,1,0:T(8,128)S(1)} %get-tuple-element.47), channel_id=1, source_target_pairs={{0,16},{16,0},{32,48},{48,32},{64,80},{80,64},{96,112},{112,96},{1... | collective-permute-start | bytes 393224 | tf_op jit(solution)/shard_map/ppermute | solution.py:192
